TPU v7x, 256 devices: a whole 4x4x8 slice. The times are simulated.
256 devices in a mesh: depth: 32 (over y, z_lo, core), sample: 4 (over x), filter: 2 (over z_hi).
Axes of the slice: x: 4, y: 4, z: 8 (z_hi: 2, z_lo: 4; z = z_hi * 4 + z_lo), core: 2. Of those that a mesh axis runs over, the one named last changes fastest.
Arguments:
- inputs: float32 [4, 64, 8, 8, 256], P('sample', 'depth', None, None, 'filter'), may hold values from -6 to 6
- pre_gelu: float32 [4, 64, 8, 8, 256], P('sample', 'depth', None, None, 'filter'), may hold values from -6 to 6
- output_grad: float32 [4, 64, 8, 8, 256], P('sample', 'depth', None, None, 'filter'), may hold values from -6 to 6
- first_weight: float32 [27, 256, 256], P(None, None, 'filter'), may hold values from -0.078125 to 0.078125
- second_weight: float32 [27, 256, 256], P(None, None, 'filter'), may hold values from -0.078125 to 0.078125
Outputs:
- input_grad: float32 [4, 64, 8, 8, 256], P('sample', 'depth', None, None, 'filter')
- first_weight_grad: float32 [27, 256, 256], P(None, 'depth', 'filter')
- second_weight_grad: float32 [27, 256, 256], P(None, 'depth', 'filter')
All inputs are finite; a program needn't handle non-finite values.
Results may differ from a plain program's by a relative error of at most 0.000098.
Values sent between devices are 32-bit elements; how exact they have to be, the bound alone decides.
A program may use at most 64 MiB of HBM per device.

v0:
```python
import math

import jax
import jax.numpy as jnp
from jax import lax
from jax.sharding import Mesh
from jax.sharding import PartitionSpec as P

DEPTH = ("depth_0", "depth_1", "depth_2")


highest = lax.Precision.HIGHEST


def padded_2(cells, sides, width):
    for axis, dim in sides:
        count = lax.axis_size(axis)
        ends = count - 1
        head = lax.slice_in_dim(cells, 0, width, axis=dim)
        tail = lax.slice_in_dim(cells, cells.shape[dim] - width, cells.shape[dim], axis=dim)
        cells = jnp.concatenate(
            [
                lax.ppermute(tail, axis, [(i, (i + 1) % count) for i in range(ends)]),
                cells,
                lax.ppermute(head, axis, [((i + 1) % count, i) for i in range(ends)]),
            ],
            axis=dim,
        )
    return cells


def cut_along(array, dim, peers):
    shape = array.shape
    tiles = array.reshape(*shape[:dim], peers, shape[dim] // peers, *shape[dim + 1 :])
    return jnp.moveaxis(tiles, dim, 0)


def summed_on_arrival(array, axis, dim):
    peers = lax.axis_size(axis)
    tiles = lax.all_to_all(cut_along(array, dim, peers), axis, 0, 0, tiled=True)
    return jnp.sum(tiles, axis=0)


def sum_by_axis(array, axes, dim):
    far, near = axes
    own = summed_on_arrival(cut_along(array, dim, lax.axis_size(far)), near, dim + 1)
    return jnp.sum(lax.all_to_all(own, far, 0, 0, tiled=True), axis=0)


def from_everyone(array, axis):
    peers = lax.axis_size(axis)
    return lax.all_to_all(
        jnp.broadcast_to(array[None], (peers, *array.shape)), axis, 0, 0, tiled=True
    )


def over_copies(array, axis):
    everything = from_everyone(array, axis)
    return jnp.sum(everything, axis=0)


def joined_along(tiles, dim):
    shape = list(tiles.shape[1:])
    shape[dim] *= tiles.shape[0]
    return jnp.moveaxis(tiles, 0, dim).reshape(shape)


def gather_directly(array, axis, dim):
    tiles = from_everyone(array, axis)
    return joined_along(tiles, dim)


def gelu_pair(pre):
    normal_cdf = 0.5 * (1.0 + lax.erf(pre * 0.7071067811865476))
    density = jnp.exp(-0.5 * pre * pre) * 0.3989422804014327
    return (pre * normal_cdf, normal_cdf + pre * density)


def pad_sides(field):
    return jnp.pad(field, [(0, 0)] * (field.ndim - 3) + [(1, 1), (1, 1), (0, 0)])


def patches(padded, flipped):
    planes = padded.shape[-4] - 2
    height = padded.shape[-3] - 2
    breadth = padded.shape[-2] - 2
    pieces = []
    for depth_tap in range(3):
        for row_tap in range(3):
            for column_tap in range(3):
                start_plane = 2 - depth_tap if flipped else depth_tap
                start_row = 2 - row_tap if flipped else row_tap
                start_column = 2 - column_tap if flipped else column_tap
                pieces.append(
                    padded[
                        ...,
                        start_plane : start_plane + planes,
                        start_row : start_row + height,
                        start_column : start_column + breadth,
                        :,
                    ]
                )
    stacked = jnp.stack(pieces, axis=-2)
    return stacked.reshape(-1, 27, padded.shape[-1])


def spread_back(grad_local, kernel):
    planes = padded_2(grad_local, ((DEPTH, 1),), 1)
    columns = patches(pad_sides(planes), True)
    partial_value = jnp.einsum("rtc,tic->ri", columns, kernel, precision=highest)
    partial_value = partial_value.reshape(grad_local.shape[:4] + (kernel.shape[1],))
    return summed_on_arrival(partial_value, "filter", 4)


def reduce_weight(raw_pair):
    shares = jax.tree.map(
        lambda part: sum_by_axis(part, (("depth_0", "depth_1"), "depth_2"), 1), raw_pair
    )
    return jax.tree.map(lambda part: over_copies(part, "sample"), shares)


def local(inputs, pre_gelu, output_grad, first_weight, second_weight):
    activated, slope = gelu_pair(pre_gelu)
    stacked = jnp.stack([inputs, activated], axis=0)
    channels = gather_directly(stacked, "filter", 5)
    whole = padded_2(channels, ((DEPTH, 2),), 1)
    padded = pad_sides(whole)
    local_width = output_grad.shape[4]
    act_columns = patches(padded[1], False)
    second_raw = jnp.einsum(
        "rti,rc->tic", act_columns, output_grad.reshape(-1, local_width), precision=highest
    )
    act_grad = spread_back(output_grad, second_weight)
    pre_grad = act_grad * slope
    input_grad = spread_back(pre_grad, first_weight)
    input_columns = patches(padded[0], False)
    first_raw = jnp.einsum(
        "rti,rc->tic", input_columns, pre_grad.reshape(-1, local_width), precision=highest
    )
    first_sum, second_sum = reduce_weight((first_raw, second_raw))
    cells = (
        inputs.shape[0]
        * lax.axis_size("sample")
        * inputs.shape[1]
        * lax.axis_size(DEPTH)
        * inputs.shape[2]
        * inputs.shape[3]
    )
    factor = 1.0 / math.sqrt(cells)
    return (input_grad, first_sum * factor, second_sum * factor)


def solution(mesh):
    finer = Mesh(
        mesh.devices.reshape(4, 4, 2, mesh.shape["sample"], mesh.shape["filter"]),
        ("depth_0", "depth_1", "depth_2", "sample", "filter"),
    )
    return jax.shard_map(
        local,
        mesh=finer,
        in_specs=(
            P("sample", DEPTH, None, None, "filter"),
            P("sample", DEPTH, None, None, "filter"),
            P("sample", DEPTH, None, None, "filter"),
            P(None, None, "filter"),
            P(None, None, "filter"),
        ),
        out_specs=(
            P("sample", DEPTH, None, None, "filter"),
            P(None, DEPTH, "filter"),
            P(None, DEPTH, "filter"),
        ),
        check_vma=False,
    )
```

profile of v0, /device:TPU:8, one launch (start us, length us, event | category | flops | bytes accessed | tf_op | source)
XLA Modules:
  0.0 254.4 jit_solution(2408526219689005924)
XLA Ops:
  3.6 6.3 %collective-permute-start.1 = (f32[1,1,8,8,128]{4,3,2,1,0:T(8,128)S(1)}, f32[1,1,8,8,128]{4,3,2,1,0:T(8,128)S(1)}, u32[]{:S(2)}, u32[]{:S(2)}) collective-permute-start(f32[1,1,8,8,128]{4,3,2,1,0:T(8,128)S(1)} %get-tuple-element.118), channel_id=1, source_target_pairs={{8,0},{16,8},{24,16},{32,24},{40,32},{48,40},{56,48},{64,56},{72,6... | collective-permute-start | bytes 98312 | tf_op jit(solution)/shard_map/ppermute | solution.py:25
  13.7 3.4 %fusion.9 = f32[2,1,2,8,8,128]{5,4,0,3,2,1:T(8,128)S(1)} fusion(f32[2,128,128,27,1,1]{2,1,0,3,5,4:T(8,128)S(1)} %bitcast.189, f32[2,8,8,128,27,1]{3,2,1,0,4,5:T(8,128)S(1)} %bitcast.308), kind=kOutput, calls=%fused_computation.19 | convolution fusion | flops 1358954496 | bytes 5439488 | tf_op jit(solution)/shard_map/rtc,tic->ri/dot_general | solution.py:110
  17.0 16.6 %all_to_all.45 = f32[2,1,2,8,8,128]{5,4,3,2,1,0:T(8,128)S(1)} all-to-all(f32[2,1,2,8,8,128]{5,4,3,2,1,0:T(8,128)S(1)} %copy.47), channel_id=1, replica_groups=mesh['depth_0'=4,'depth_1'=4,'depth_2'=2,'sample'=4,'filter'=2] {'filter'}, dimensions={0} | all-to-all | bytes 262144 | tf_op jit(solution)/shard_map/all_to_all | solution.py:40
  36.5 6.3 %collective-permute-start.3 = (f32[1,1,8,8,128]{4,3,2,1,0:T(8,128)S(1)}, f32[1,1,8,8,128]{4,3,2,1,0:T(8,128)S(1)}, u32[]{:S(2)}, u32[]{:S(2)}) collective-permute-start(f32[1,1,8,8,128]{4,3,2,1,0:T(8,128)S(1)} %get-tuple-element.114), channel_id=1, source_target_pairs={{8,0},{16,8},{24,16},{32,24},{40,32},{48,40},{56,48},{64,56},{72,6... | collective-permute-start | bytes 98312 | tf_op jit(solution)/shard_map/ppermute | solution.py:25
  44.5 3.4 %all-to-all-start.2 = ((f32[2,2,1,2,8,8,128]{6,5,4,3,1,2,0:T(8,128)}), f32[2,2,1,2,8,8,128]{6,5,4,3,1,2,0:T(8,128)S(1)}, u32[]{:S(2)}, u32[]{:S(2)}) async-start(f32[2,2,1,2,8,8,128]{6,5,4,3,1,2,0:T(8,128)} %broadcast_in_dim.9), calls=%async_computation.2 | async-start | bytes 524288 | tf_op jit(solution)/shard_map/all_to_all | solution.py:52
  67.1 6.5 %collective-permute-start.5 = (f32[2,1,1,8,8,256]{5,4,3,2,1,0:T(8,128)S(1)}, f32[2,1,1,8,8,256]{5,4,3,2,1,0:T(8,128)S(1)}, u32[]{:S(2)}, u32[]{:S(2)}) collective-permute-start(f32[2,1,1,8,8,256]{5,4,3,2,1,0:T(8,128)S(1)} %get-tuple-element.108), channel_id=1, source_target_pairs={{8,0},{16,8},{24,16},{32,24},{40,32},{48,40},{56,48},{64,56},{72,6... | collective-permute-start | bytes 393224 | tf_op jit(solution)/shard_map/ppermute | solution.py:25
  73.7 5.9 %fusion.14 = f32[2,1,2,8,8,128]{5,4,0,3,2,1:T(8,128)S(1)} fusion(f32[2,128,128,27,1,1]{2,1,0,3,5,4:T(8,128)} %bitcast.309, f32[2,8,8,128,27,1]{3,2,1,0,4,5:T(8,128)} %bitcast.67), kind=kOutput, calls=%fused_computation.20 | convolution fusion | flops 1358954496 | bytes 5439488 | tf_op jit(solution)/shard_map/rtc,tic->ri/dot_general | solution.py:110
  85.6 3.3 %copy.56 = f32[27,256,128]{2,1,0:T(8,128)S(1)} copy(f32[27,256,128]{1,2,0:T(8,128)} %bitcast.194) | data formatting | bytes 7077888 | tf_op jit(solution)/shard_map/rti,rc->tic/dot_general | solution.py:130
  88.9 3.9 %convolution_bitcast_fusion = f32[16,27,2,8,128]{4,3,2,0,1:T(8,128)S(1)} fusion(f32[27,16,16,128]{3,2,1,0:T(8,128)S(1)} %bitcast.192, f32[128,128,1,1]{1,0,3,2:T(8,128)} %bitcast.198), kind=kOutput, calls=%fused_computation.6 | convolution fusion | flops 1358954496 | bytes 7143424 | tf_op jit(solution)/shard_map/rti,rc->tic/dot_general | solution.py:130
  93.3 6.6 %all_to_all.46 = f32[2,16,27,8,128]{4,3,1,2,0:T(8,128)S(1)} all-to-all(f32[2,16,27,8,128]{4,3,1,2,0:T(8,128)S(1)} %bitcast.193), channel_id=1, replica_groups=mesh['depth_0'=4,'depth_1'=4,'depth_2'=2,'sample'=4,'filter'=2] {'depth_2'}, dimensions={0} | all-to-all | bytes 7077888 | tf_op jit(solution)/shard_map/all_to_all | solution.py:40
  99.9 7.2 %all-to-all-start.1 = ((f32[2,1,2,8,8,128]{5,4,3,2,1,0:T(8,128)}), f32[2,1,2,8,8,128]{5,4,3,2,1,0:T(8,128)}, u32[]{:S(2)}, u32[]{:S(2)}) async-start(f32[2,1,2,8,8,128]{5,4,3,2,1,0:T(8,128)} %copy.50), calls=%async_computation.1 | async-start | bytes 262144 | tf_op jit(solution)/shard_map/all_to_all | solution.py:40
  108.7 2.9 %copy.59 = f32[16,27,8,128]{3,2,1,0:T(8,128)} copy(f32[16,27,8,128]{3,2,0,1:T(8,128)} %reduce_sum.83) | data formatting | bytes 3538944 | tf_op jit(solution)/shard_map/reduce_sum | solution.py:41
  115.7 3.3 %copy.52 = f32[27,256,128]{2,1,0:T(8,128)S(1)} copy(f32[27,256,128]{1,2,0:T(8,128)} %bitcast.195) | data formatting | bytes 7077888 | tf_op jit(solution)/shard_map/rti,rc->tic/dot_general | solution.py:137
  119.0 3.9 %convolution_bitcast_fusion.1 = f32[16,27,2,8,128]{4,3,2,0,1:T(8,128)S(1)} fusion(f32[27,16,16,128]{3,2,1,0:T(8,128)S(1)} %bitcast.191, f32[128,128,1,1]{1,0,3,2:T(8,128)} %bitcast.197), kind=kOutput, calls=%fused_computation.7 | convolution fusion | flops 1358954496 | bytes 7143424 | tf_op jit(solution)/shard_map/rti,rc->tic/dot_general | solution.py:137
  123.3 7.6 %all_to_all.47 = f32[2,16,27,8,128]{4,3,1,2,0:T(8,128)} all-to-all(f32[2,16,27,8,128]{4,3,1,2,0:T(8,128)S(1)} %bitcast.190), channel_id=1, replica_groups=mesh['depth_0'=4,'depth_1'=4,'depth_2'=2,'sample'=4,'filter'=2] {'depth_2'}, dimensions={0} | all-to-all | bytes 7077888 | tf_op jit(solution)/shard_map/all_to_all | solution.py:40
  130.9 5.2 %all-to-all-start.7 = ((f32[16,27,8,128]{3,2,1,0:T(8,128)}), f32[16,27,8,128]{3,2,1,0:T(8,128)}, u32[]{:S(2)}, u32[]{:S(2)}) async-start(f32[16,27,8,128]{3,2,1,0:T(8,128)} %copy.59), calls=%async_computation.7 | async-start | bytes 3538944 | tf_op jit(solution)/shard_map/all_to_all | solution.py:47
  137.8 2.8 %copy.55 = f32[16,27,8,128]{3,2,1,0:T(8,128)} copy(f32[16,27,8,128]{3,2,0,1:T(8,128)} %reduce_sum.80) | data formatting | bytes 3538944 | tf_op jit(solution)/shard_map/reduce_sum | solution.py:41
  140.6 36.6 %all-to-all-done.7 = f32[16,27,8,128]{3,2,1,0:T(8,128)} async-done(((f32[16,27,8,128]{3,2,1,0:T(8,128)}), f32[16,27,8,128]{3,2,1,0:T(8,128)}, u32[]{:S(2)}, u32[]{:S(2)}) %all-to-all-start.7) | async-done | bytes 1769504 | tf_op jit(solution)/shard_map/all_to_all | solution.py:47
  177.2 6.9 %all-to-all-start.4 = ((f32[16,27,8,128]{3,2,1,0:T(8,128)}), f32[16,27,8,128]{3,2,1,0:T(8,128)}, u32[]{:S(2)}, u32[]{:S(2)}) async-start(f32[16,27,8,128]{3,2,1,0:T(8,128)} %copy.55), calls=%async_computation.4 | async-start | bytes 3538944 | tf_op jit(solution)/shard_map/all_to_all | solution.py:47
  185.7 38.7 %all-to-all-done.4 = f32[16,27,8,128]{3,2,1,0:T(8,128)} async-done(((f32[16,27,8,128]{3,2,1,0:T(8,128)}), f32[16,27,8,128]{3,2,1,0:T(8,128)}, u32[]{:S(2)}, u32[]{:S(2)}) %all-to-all-start.4) | async-done | bytes 1769504 | tf_op jit(solution)/shard_map/all_to_all | solution.py:47
  225.2 4.3 %all-to-all-start.8 = ((f32[4,27,8,128]{3,2,1,0:T(8,128)}), f32[4,27,8,128]{3,2,1,0:T(8,128)}, u32[]{:S(2)}, u32[]{:S(2)}) async-start(f32[4,27,8,128]{3,2,1,0:T(8,128)} %broadcast_in_dim.11), calls=%async_computation.8 | async-start | bytes 884736 | tf_op jit(solution)/shard_map/all_to_all | solution.py:52
  231.9 5.7 %all-to-all-done.8 = f32[4,27,8,128]{3,2,1,0:T(8,128)} async-done(((f32[4,27,8,128]{3,2,1,0:T(8,128)}), f32[4,27,8,128]{3,2,1,0:T(8,128)}, u32[]{:S(2)}, u32[]{:S(2)}) %all-to-all-start.8) | async-done | bytes 442400 | tf_op jit(solution)/shard_map/all_to_all | solution.py:52
  239.3 4.1 %all-to-all-start.5 = ((f32[4,27,8,128]{3,2,1,0:T(8,128)}), f32[4,27,8,128]{3,2,1,0:T(8,128)}, u32[]{:S(2)}, u32[]{:S(2)}) async-start(f32[4,27,8,128]{3,2,1,0:T(8,128)} %broadcast_in_dim.10), calls=%async_computation.5 | async-start | bytes 884736 | tf_op jit(solution)/shard_map/all_to_all | solution.py:52
  248.2 2.9 %all-to-all-done.5 = f32[4,27,8,128]{3,2,1,0:T(8,128)} async-done(((f32[4,27,8,128]{3,2,1,0:T(8,128)}), f32[4,27,8,128]{3,2,1,0:T(8,128)}, u32[]{:S(2)}, u32[]{:S(2)}) %all-to-all-start.5) | async-done | bytes 442400 | tf_op jit(solution)/shard_map/all_to_all | solution.py:52
  (223 shorter events, 58.3 us)
Async XLA Ops:
  0.6 13.0 %copy-start = (f32[27,256,128]{2,1,0:T(8,128)S(1)}, f32[27,256,128]{2,1,0:T(8,128)}, u32[]{:S(2)}) copy-start(f32[27,256,128]{2,1,0:T(8,128)} %param.9) | copy-start | bytes 10616836
  1.6 8.4 %collective-permute-start = (f32[1,1,8,8,128]{4,3,2,1,0:T(8,128)S(1)}, f32[1,1,8,8,128]{4,3,2,1,0:T(8,128)S(1)}, u32[]{:S(2)}, u32[]{:S(2)}) collective-permute-start(f32[1,1,8,8,128]{4,3,2,1,0:T(8,128)S(1)} %get-tuple-element.117), channel_id=1, source_target_pairs={{0,8},{8,16},{16,24},{24,32},{32,40},{40,48},{48,56},{56,64},{64,7... | collective-permute-start | bytes 98312 | tf_op jit(solution)/shard_map/ppermute | solution.py:23
  3.6 7.9 %collective-permute-start.1 = (f32[1,1,8,8,128]{4,3,2,1,0:T(8,128)S(1)}, f32[1,1,8,8,128]{4,3,2,1,0:T(8,128)S(1)}, u32[]{:S(2)}, u32[]{:S(2)}) collective-permute-start(f32[1,1,8,8,128]{4,3,2,1,0:T(8,128)S(1)} %get-tuple-element.118), channel_id=1, source_target_pairs={{8,0},{16,8},{24,16},{32,24},{40,32},{48,40},{56,48},{64,56},{72,6... | collective-permute-start | bytes 98312 | tf_op jit(solution)/shard_map/ppermute | solution.py:25
  34.6 21.8 %copy-start.5 = (f32[1,2,8,8,128]{4,3,2,1,0:T(8,128)}, f32[1,2,8,8,128]{4,3,2,1,0:T(8,128)S(1)}, u32[]{:S(2)}) copy-start(f32[1,2,8,8,128]{4,3,2,1,0:T(8,128)S(1)} %get-tuple-element.110) | copy-start | bytes 196612
  34.6 13.3 %collective-permute-start.2 = (f32[1,1,8,8,128]{4,3,2,1,0:T(8,128)S(1)}, f32[1,1,8,8,128]{4,3,2,1,0:T(8,128)S(1)}, u32[]{:S(2)}, u32[]{:S(2)}) collective-permute-start(f32[1,1,8,8,128]{4,3,2,1,0:T(8,128)S(1)} %get-tuple-element.113), channel_id=1, source_target_pairs={{0,8},{8,16},{16,24},{24,32},{32,40},{40,48},{48,56},{56,64},{64,7... | collective-permute-start | bytes 98312 | tf_op jit(solution)/shard_map/ppermute | solution.py:23
  36.5 11.4 %collective-permute-start.3 = (f32[1,1,8,8,128]{4,3,2,1,0:T(8,128)S(1)}, f32[1,1,8,8,128]{4,3,2,1,0:T(8,128)S(1)}, u32[]{:S(2)}, u32[]{:S(2)}) collective-permute-start(f32[1,1,8,8,128]{4,3,2,1,0:T(8,128)S(1)} %get-tuple-element.114), channel_id=1, source_target_pairs={{8,0},{16,8},{24,16},{32,24},{40,32},{48,40},{56,48},{64,56},{72,6... | collective-permute-start | bytes 98312 | tf_op jit(solution)/shard_map/ppermute | solution.py:25
  44.5 20.7 %all-to-all-start.2 = ((f32[2,2,1,2,8,8,128]{6,5,4,3,1,2,0:T(8,128)}), f32[2,2,1,2,8,8,128]{6,5,4,3,1,2,0:T(8,128)S(1)}, u32[]{:S(2)}, u32[]{:S(2)}) async-start(f32[2,2,1,2,8,8,128]{6,5,4,3,1,2,0:T(8,128)} %broadcast_in_dim.9), calls=%async_computation.2 | async-start | bytes 524288 | tf_op jit(solution)/shard_map/all_to_all | solution.py:52
  65.2 15.0 %collective-permute-start.4 = (f32[2,1,1,8,8,256]{5,4,3,2,1,0:T(8,128)S(1)}, f32[2,1,1,8,8,256]{5,4,3,2,1,0:T(8,128)S(1)}, u32[]{:S(2)}, u32[]{:S(2)}) collective-permute-start(f32[2,1,1,8,8,256]{5,4,3,2,1,0:T(8,128)S(1)} %get-tuple-element.107), channel_id=1, source_target_pairs={{0,8},{8,16},{16,24},{24,32},{32,40},{40,48},{48,56},{56,64},{64,7... | collective-permute-start | bytes 393224 | tf_op jit(solution)/shard_map/ppermute | solution.py:23
  67.1 13.1 %collective-permute-start.5 = (f32[2,1,1,8,8,256]{5,4,3,2,1,0:T(8,128)S(1)}, f32[2,1,1,8,8,256]{5,4,3,2,1,0:T(8,128)S(1)}, u32[]{:S(2)}, u32[]{:S(2)}) collective-permute-start(f32[2,1,1,8,8,256]{5,4,3,2,1,0:T(8,128)S(1)} %get-tuple-element.108), channel_id=1, source_target_pairs={{8,0},{16,8},{24,16},{32,24},{40,32},{48,40},{56,48},{64,56},{72,6... | collective-permute-start | bytes 393224 | tf_op jit(solution)/shard_map/ppermute | solution.py:25
  83.8 1.8 copy-start.3
  99.9 23.5 %all-to-all-start.1 = ((f32[2,1,2,8,8,128]{5,4,3,2,1,0:T(8,128)}), f32[2,1,2,8,8,128]{5,4,3,2,1,0:T(8,128)}, u32[]{:S(2)}, u32[]{:S(2)}) async-start(f32[2,1,2,8,8,128]{5,4,3,2,1,0:T(8,128)} %copy.50), calls=%async_computation.1 | async-start | bytes 262144 | tf_op jit(solution)/shard_map/all_to_all | solution.py:40
  108.7 3.0 %copy-start.33 = (f32[1,2,8,8,256]{4,3,2,1,0:T(8,128)S(1)}, f32[1,2,8,8,256]{4,3,2,1,0:T(8,128)}, u32[]{:S(2)}) copy-start(f32[1,2,8,8,256]{4,3,2,1,0:T(8,128)} %get-tuple-element.119) | copy-start | bytes 393220
  108.7 3.1 %copy-start.32 = (f32[1,2,8,8,256]{4,3,2,1,0:T(8,128)S(1)}, f32[1,2,8,8,256]{4,3,2,1,0:T(8,128)}, u32[]{:S(2)}) copy-start(f32[1,2,8,8,256]{4,3,2,1,0:T(8,128)} %get-tuple-element.120) | copy-start | bytes 393220
  108.7 3.1 %copy-start.31 = (f32[1,2,8,8,256]{4,3,2,1,0:T(8,128)S(1)}, f32[1,2,8,8,256]{4,3,2,1,0:T(8,128)}, u32[]{:S(2)}) copy-start(f32[1,2,8,8,256]{4,3,2,1,0:T(8,128)} %get-tuple-element.121) | copy-start | bytes 393220
  108.7 3.1 %copy-start.30 = (f32[1,2,8,8,256]{4,3,2,1,0:T(8,128)S(1)}, f32[1,2,8,8,256]{4,3,2,1,0:T(8,128)}, u32[]{:S(2)}) copy-start(f32[1,2,8,8,256]{4,3,2,1,0:T(8,128)} %get-tuple-element.122) | copy-start | bytes 393220
  108.7 3.2 %copy-start.29 = (f32[1,2,8,8,256]{4,3,2,1,0:T(8,128)S(1)}, f32[1,2,8,8,256]{4,3,2,1,0:T(8,128)}, u32[]{:S(2)}) copy-start(f32[1,2,8,8,256]{4,3,2,1,0:T(8,128)} %get-tuple-element.123) | copy-start | bytes 393220
  108.7 3.2 %copy-start.28 = (f32[1,2,8,8,256]{4,3,2,1,0:T(8,128)S(1)}, f32[1,2,8,8,256]{4,3,2,1,0:T(8,128)}, u32[]{:S(2)}) copy-start(f32[1,2,8,8,256]{4,3,2,1,0:T(8,128)} %get-tuple-element.124) | copy-start | bytes 393220
  108.7 3.2 %copy-start.27 = (f32[1,2,8,8,256]{4,3,2,1,0:T(8,128)S(1)}, f32[1,2,8,8,256]{4,3,2,1,0:T(8,128)}, u32[]{:S(2)}) copy-start(f32[1,2,8,8,256]{4,3,2,1,0:T(8,128)} %get-tuple-element.125) | copy-start | bytes 393220
  130.9 5.2 %copy-start.2 = (f32[2,16,27,8,128]{4,3,1,2,0:T(8,128)S(1)}, f32[2,16,27,8,128]{4,3,1,2,0:T(8,128)}, u32[]{:S(2)}) copy-start(f32[2,16,27,8,128]{4,3,1,2,0:T(8,128)} %all_to_all.47) | copy-start | bytes 10616836
  130.9 46.3 %all-to-all-start.7 = ((f32[16,27,8,128]{3,2,1,0:T(8,128)}), f32[16,27,8,128]{3,2,1,0:T(8,128)}, u32[]{:S(2)}, u32[]{:S(2)}) async-start(f32[16,27,8,128]{3,2,1,0:T(8,128)} %copy.59), calls=%async_computation.7 | async-start | bytes 3538944 | tf_op jit(solution)/shard_map/all_to_all | solution.py:47
  177.2 47.2 %all-to-all-start.4 = ((f32[16,27,8,128]{3,2,1,0:T(8,128)}), f32[16,27,8,128]{3,2,1,0:T(8,128)}, u32[]{:S(2)}, u32[]{:S(2)}) async-start(f32[16,27,8,128]{3,2,1,0:T(8,128)} %copy.55), calls=%async_computation.4 | async-start | bytes 3538944 | tf_op jit(solution)/shard_map/all_to_all | solution.py:47
  225.2 12.3 %all-to-all-start.8 = ((f32[4,27,8,128]{3,2,1,0:T(8,128)}), f32[4,27,8,128]{3,2,1,0:T(8,128)}, u32[]{:S(2)}, u32[]{:S(2)}) async-start(f32[4,27,8,128]{3,2,1,0:T(8,128)} %broadcast_in_dim.11), calls=%async_computation.8 | async-start | bytes 884736 | tf_op jit(solution)/shard_map/all_to_all | solution.py:52
  229.5 24.8 %copy-start.1 = (f32[27,256,128]{2,1,0:T(8,128)S(1)}, f32[27,256,128]{2,1,0:T(8,128)}, u32[]{:S(2)}) copy-start(f32[27,256,128]{2,1,0:T(8,128)} %param.9) | copy-start | bytes 10616836
  239.3 11.8 %all-to-all-start.5 = ((f32[4,27,8,128]{3,2,1,0:T(8,128)}), f32[4,27,8,128]{3,2,1,0:T(8,128)}, u32[]{:S(2)}, u32[]{:S(2)}) async-start(f32[4,27,8,128]{3,2,1,0:T(8,128)} %broadcast_in_dim.10), calls=%async_computation.5 | async-start | bytes 884736 | tf_op jit(solution)/shard_map/all_to_all | solution.py:52
  (22 other events, 25.1 us)
where the time goes:
time: 257 us; the launch traced here: 254 us
  waiting for transfers between devices  85.5 us (33%)
  starting transfers between devices  56.2 us (22%)
  local copies, waits for them, and re-layouts  45 us (18%)
  blocking collectives  30.8 us (12%)
  other arithmetic  18.1 us (7%)
  matrix products  16.9 us (7%)
    all_to_all x2, waiting for transfers between devices, sum_by_axis(): return jnp.sum(lax.all_to_all(own, far, 0, 0, tiled=True), axis=0)  75.3 us
    all_to_all x3, blocking collectives, summed_on_arrival(): tiles = lax.all_to_all(cut_along(array, dim, peers), axis, 0, 0, tiled=True)  30.8 us
    unnamed x172, local copies, waits for them, and re-layouts  23.1 us
    ppermute x3, starting transfers between devices, padded_2(): lax.ppermute(head, axis, [((i + 1) % count, i) for i in range(ends)])  19.2 us
    all_to_all x2, starting transfers between devices, sum_by_axis(): return jnp.sum(lax.all_to_all(own, far, 0, 0, tiled=True), axis=0)  12.1 us
    all_to_all x3, starting transfers between devices, from_everyone(): lax.all_to_all(jnp.broadcast_to(array[None], (peers, *array.shape)), axis...  11.9 us
    dot_general x2, matrix products, spread_back(): jnp.einsum('rtc,tic->ri', columns, kernel, precision=highest)  9.23 us
    all_to_all x3, waiting for transfers between devices, from_everyone(): lax.all_to_all(jnp.broadcast_to(array[None], (peers, *array.shape)), axis...  8.6 us
  transfers between devices with their start and end apart: 12, of which 5 were waited for; matrix products, arithmetic and copies ran while one was open for 20% of the time, Pallas kernels for 0%

commit v1 on v0

v1 whole, which is shorter than its diff:
```python
import jax
import jax.numpy as jnp
from jax import lax
from jax.experimental import pallas as pl
from jax.experimental.pallas import tpu as pltpu
from jax.sharding import PartitionSpec as P

F32 = jnp.float32
BF16 = jnp.bfloat16
TAPS = 27
ROWS = TAPS * 8
K_CONV = TAPS * 128
THIRD = 9 * 128


def remote(src, dst, send, recv, device):
    return pltpu.make_async_remote_copy(
        src_ref=src,
        dst_ref=dst,
        send_sem=send,
        recv_sem=recv,
        device_id=device,
        device_id_type=pl.DeviceIdType.MESH,
    )


def gelu_pair(pre):
    normal_cdf = 0.5 * (1.0 + lax.erf(pre * 0.7071067811865476))
    density = jnp.exp(-0.5 * pre * pre) * 0.3989422804014327
    return pre * normal_cdf, normal_cdf + pre * density


def parts_of(value):
    high = value.astype(BF16)
    return high, (value - high.astype(F32)).astype(BF16)


def lanes_of(rows):
    return lax.broadcasted_iota(jnp.int32, (rows, 128), 1)


def moved(base, dh, dw):
    if dh == 0 and dw == 0:
        return base
    lane = lanes_of(base.shape[0])
    h = (lane // 8) % 8 + dh
    w = lane % 8 + dw
    inside = (h >= 0) & (h < 8) & (w >= 0) & (w < 8)
    return jnp.where(inside, pltpu.roll(base, (-(dh * 8 + dw)) % 128, 1), 0.0)


def kernel(
    inp_hbm, pre_hbm, og_hbm, w1_hbm, w2_hbm,
    grad_out, first_out, second_out,
    og_v, pre_v, inp_v, wf, wb1, wb2, cols, acc,
    og_halo, pg_halo, pair_pre, pair_inp, slope_v, field_t, slices, owned, low_act, high_act,
    og_all, pg_all, rhs, lhs, part_out, part_in, pgt_v, pg_v,
    y_out, y_in, y_sum, z_out, z_in, x_all, x_out,
    load_sem, halo_s, halo_r, pair_s, pair_r, ring_s, ring_r, slice_s, slice_r, edge_s, edge_r,
    y_s, y_r, z_s, z_r, x_s, x_r,
):
    d = lax.axis_index("depth")
    s = lax.axis_index("sample")
    f = lax.axis_index("filter")
    c = d % 2
    chip = d // 2
    zl = chip % 4
    y = d // 8
    partner = d + 1 - 2 * c

    to_filter = (d, s, 1 - f)
    group = [(0, 1)] + [(k, o) for k in (2, 1, 3) for o in (0, 1)]

    def group_device(k, o):
        return (partner if o else d, (s + k) % 4, f)

    to_next, to_last = ((d + 1) % 32, s, f), ((d + 31) % 32, s, f)
    to_next_chip, to_last_chip = ((d + 2) % 32, s, f), ((d + 30) % 32, s, f)

    def to_y(k):
        return ((d + 8 * k) % 32, s, f)

    def to_z(k):
        return (y * 8 + ((zl + k) % 4) * 2 + c, s, f)

    loads = [
        pltpu.make_async_copy(og_hbm, og_v, load_sem.at[0]),
        pltpu.make_async_copy(pre_hbm, pre_v, load_sem.at[1]),
        pltpu.make_async_copy(inp_hbm, inp_v, load_sem.at[2]),
        pltpu.make_async_copy(w2_hbm, wf.at[0], load_sem.at[3]),
        pltpu.make_async_copy(w1_hbm, wf.at[1], load_sem.at[4]),
    ]
    for load in loads:
        load.start()

    barrier = pltpu.get_barrier_semaphore()
    friends = [to_filter, to_next, to_last, to_next_chip, to_last_chip]
    friends += [group_device(k, o) for k, o in group]
    friends += [to_y(k) for k in (1, 2, 3)] + [to_z(k) for k in (1, 2, 3)]
    for friend in friends:
        pl.semaphore_signal(barrier, inc=1, device_id=friend, device_id_type=pl.DeviceIdType.MESH)

    started = []

    def send(*args):
        copy = remote(*args)
        copy.start()
        started.append(copy)
        return copy

    lane = lanes_of(128)
    left = lane < 64

    def patch(base, depth_tap):
        for b in range(3):
            for e in range(3):
                t = 9 * depth_tap + 3 * b + e
                high, low = parts_of(moved(base, 1 - b, 1 - e))
                cols[t * 128 : (t + 1) * 128, 0:128] = high
                cols[t * 128 : (t + 1) * 128, 128:256] = low

    def patch_edges(own, halo_ref):
        edge = halo_ref[...].T
        edge = jnp.where(left & (d == 0), 0.0, edge)
        edge = jnp.where((~left) & (d == 31), 0.0, edge)
        swapped = pltpu.roll(own, 64, 1)
        patch(jnp.where(left, swapped, edge), 0)
        patch(jnp.where(left, edge, swapped), 2)

    def split_weight(n, wb):
        def body(t, carry):
            at = pl.ds(pl.multiple_of(t * 128, 128), 128)
            for h in range(2):
                high, low = parts_of(wf[n, t, h * 128 : (h + 1) * 128, :])
                wb[h, 0:128, at] = high
                wb[h, 128:256, at] = low
            return carry

        lax.fori_loop(0, TAPS, body, 0)

    def product(wb, h, third):
        at = slice(third * THIRD, (third + 1) * THIRD)
        return jnp.dot(wb[h, :, at], cols[at, :], preferred_element_type=F32)

    def fold(total):
        return (total[0:128, 0:128] + total[0:128, 128:256]) + (
            total[128:256, 0:128] + total[128:256, 128:256]
        )

    def conv_middle(wb):
        for h in range(2):
            acc[h] = product(wb, h, 1)

    def conv_rest(wb, h):
        return fold(acc[h] + (product(wb, h, 0) + product(wb, h, 2)))

    loads[0].wait()
    og_t = og_v[...].T
    patch(og_t, 1)
    og_all[c, 0] = og_v[...]
    loads[1].wait()
    act_t, slope_t = gelu_pair(pre_v[...].T)
    slope_v[...] = slope_t
    field_t[0, f] = act_t
    loads[2].wait()
    field_t[1, f] = inp_v[...].T

    pl.semaphore_wait(barrier, len(friends))

    og_edges = [
        send(og_v.at[pl.ds(64, 64)], og_halo.at[pl.ds(0, 64)], halo_s.at[0], halo_r.at[0], to_next),
        send(og_v.at[pl.ds(0, 64)], og_halo.at[pl.ds(64, 64)], halo_s.at[1], halo_r.at[1], to_last),
    ]
    pairs = [
        send(pre_v, pair_pre, pair_s.at[0], pair_r.at[0], to_filter),
        send(inp_v, pair_inp, pair_s.at[1], pair_r.at[1], to_filter),
    ]

    def gather(src, dst, n):
        return [
            send(src, dst.at[c, (4 - k) % 4], ring_s.at[n, i], ring_r.at[n, i], group_device(k, o))
            for i, (k, o) in enumerate(group)
        ]

    og_gather = gather(og_v, og_all, 0)

    loads[3].wait()
    split_weight(0, wb2)
    conv_middle(wb2)
    loads[4].wait()
    split_weight(1, wb1)

    for copy in og_edges:
        copy.wait_recv()
    patch_edges(og_t, og_halo)
    part_out[0] = conv_rest(wb2, 1 - f)
    act_pair = send(part_out.at[0], part_in.at[0], pair_s.at[2], pair_r.at[2], to_filter)
    own_part = conv_rest(wb2, f)

    sliced = []
    for n, recv in ((0, pair_pre), (1, pair_inp)):
        pairs[n].wait_recv()
        other = recv[...].T
        if n == 0:
            other, _ = gelu_pair(other)
        field_t[n, 1 - f] = other
        for half in range(2):
            for core in range(2):
                for x in range(4):
                    for hi in range(2):
                        for e in range(2):
                            row = hi * 8 + e * 4
                            slices[n, core, x, half, row : row + 4, :] = field_t[
                                n, half, pl.ds(64 * hi + 8 * core + 2 * x + e, 4, stride=16), :
                            ]
        owned[n, c, 0] = slices[n, c, s]
        sliced.append(
            [
                send(
                    slices.at[n, (1 - c) if o else c, (s + k) % 4],
                    owned.at[n, c, (4 - k) % 4],
                    slice_s.at[n, i],
                    slice_r.at[n, i],
                    group_device(k, o),
                )
                for i, (k, o) in enumerate(group)
            ]
        )
    edges = []
    for n in range(2):
        for copy in sliced[n]:
            copy.wait_recv()
        edges.append(
            [
                send(owned.at[n, 1], low_act.at[n], edge_s.at[n, 0], edge_r.at[n, 0], to_next_chip),
                send(owned.at[n, 0], high_act.at[n], edge_s.at[n, 1], edge_r.at[n, 1], to_last_chip),
            ]
        )

    act_pair.wait_recv()
    pg_t = (own_part + part_in[0]) * slope_v[...]
    pgt_v[...] = pg_t
    pg_v[...] = pg_t.T
    pg_gather = gather(pg_v, pg_all, 1)
    pg_edges = [
        send(pg_v.at[pl.ds(64, 64)], pg_halo.at[pl.ds(0, 64)], halo_s.at[2], halo_r.at[2], to_next),
        send(pg_v.at[pl.ds(0, 64)], pg_halo.at[pl.ds(64, 64)], halo_s.at[3], halo_r.at[3], to_last),
    ]
    pg_all[c, 0] = pg_v[...]
    patch(pg_t, 1)
    conv_middle(wb1)

    def make_rhs(n, ref):
        high, low = parts_of(ref[...].reshape(1024, 128))
        rhs[n, :, 0:128] = high
        rhs[n, :, 128:256] = low

    def make_lhs(n):
        for copy in edges[n]:
            copy.wait_recv()
        near = lanes_of(32) < 64

        def body(k, carry):
            first = owned[n, 0, k].reshape(32, 128)
            last = owned[n, 1, k].reshape(32, 128)
            below = jnp.where(chip == 0, 0.0, low_act[n, k].reshape(32, 128))
            above = jnp.where(chip == 15, 0.0, high_act[n, k].reshape(32, 128))

            def joined(one, two):
                return pltpu.roll(jnp.where(near, two, one), 64, 1)

            middle = joined(first, last)
            bases = [
                (joined(below, first), ((0, 0),)),
                (first, ((1, 0),)),
                (middle, ((2, 0), (0, 1))),
                (last, ((1, 1),)),
                (joined(last, above), ((2, 1),)),
            ]
            for base, uses in bases:
                for b in range(3):
                    for e in range(3):
                        value = moved(base, b - 1, e - 1)
                        high = value.astype(BF16).astype(F32)
                        low = value - high
                        for yy in range(4):
                            rows = slice(yy * 8, yy * 8 + 8)
                            tile = jnp.concatenate([high[rows], low[rows]], axis=0).astype(BF16)
                            for a, core in uses:
                                t = 9 * a + 3 * b + e
                                at = pl.ds(pl.multiple_of(core * 512 + k * 128, 128), 128)
                                lhs[n, yy, t * 16 : (t + 1) * 16, at] = tile
            return carry

        lax.fori_loop(0, 4, body, 0)

    def raw_chunk(n, k):
        total = jnp.dot(lhs[n, (y + k) % 4], rhs[n], preferred_element_type=F32)
        total = (total[:, 0:128] + total[:, 128:256]).reshape(TAPS, 16, 128)
        return (total[:, 0:8] + total[:, 8:16]).reshape(ROWS, 128)

    def raw(n):
        copies = []
        for k in (2, 1, 3):
            y_out[n, k] = raw_chunk(n, k)
            copies.append(
                send(y_out.at[n, k], y_in.at[n, 4 - k], y_s.at[n, k], y_r.at[n, k], to_y(k))
            )
        y_sum[n] = raw_chunk(n, 0)
        return copies

    for copy in og_gather:
        copy.wait_recv()
    make_rhs(0, og_all)
    make_lhs(0)
    second_y = raw(0)
    make_lhs(1)
    for copy in pg_gather:
        copy.wait_recv()
    make_rhs(1, pg_all)
    first_y = raw(1)

    for copy in pg_edges:
        copy.wait_recv()
    patch_edges(pgt_v[...], pg_halo)
    part_out[1] = conv_rest(wb1, 1 - f)
    in_pair = send(part_out.at[1], part_in.at[1], pair_s.at[3], pair_r.at[3], to_filter)
    own_grad = conv_rest(wb1, f)

    for n, copies in ((0, second_y), (1, first_y)):
        for copy in copies:
            copy.wait_recv()
        y_sum[n] = (y_sum[n] + y_in[n, 1]) + (y_in[n, 2] + y_in[n, 3])
        for zz in range(4):
            z_out[zz, n, 0:54, :] = y_sum[n, pl.ds(zz, 54, stride=4), :]
            z_out[zz, n, 54:56, :] = jnp.zeros((2, 128), F32)
    z_copies = [
        send(z_out.at[(zl + k) % 4], z_in.at[4 - k], z_s.at[k], z_r.at[k], to_z(k)) for k in (1, 2, 3)
    ]
    for copy in z_copies:
        copy.wait_recv()
    x_out[...] = ((z_out[zl] + z_in[1]) + (z_in[2] + z_in[3])) * (1.0 / 128.0)
    x_copies = [
        send(x_out, x_all.at[s], x_s.at[k], x_r.at[k], (d, (s + k) % 4, f)) for k in (1, 2, 3)
    ]
    x_all[s] = x_out[...]

    in_pair.wait_recv()
    grad_out[...] = (own_grad + part_in[1]).T

    for copy in x_copies:
        copy.wait_recv()
    for n, out in ((0, second_out), (1, first_out)):
        for x in range(4):
            for e in range(2):
                out[pl.ds(2 * x + e, TAPS, stride=8), :] = x_all[x, n, pl.ds(e, TAPS, stride=2), :]

    for copy in started:
        copy.wait_send()


def local(inputs, pre_gelu, output_grad, first_weight, second_weight):
    shape = inputs.shape
    hbm = pl.BlockSpec(memory_space=pl.ANY)
    vmem = pl.BlockSpec(memory_space=pltpu.VMEM)
    dma = pltpu.SemaphoreType.DMA
    block = (128, 128)
    grad, first, second = pl.pallas_call(
        kernel,
        out_shape=(
            jax.ShapeDtypeStruct(block, F32),
            jax.ShapeDtypeStruct((ROWS, 128), F32),
            jax.ShapeDtypeStruct((ROWS, 128), F32),
        ),
        in_specs=[hbm] * 5,
        out_specs=(vmem, vmem, vmem),
        scratch_shapes=[
            pltpu.VMEM(block, F32),
            pltpu.VMEM(block, F32),
            pltpu.VMEM(block, F32),
            pltpu.VMEM((2, TAPS, 256, 128), F32),
            pltpu.VMEM((2, 256, K_CONV), BF16),
            pltpu.VMEM((2, 256, K_CONV), BF16),
            pltpu.VMEM((K_CONV, 256), BF16),
            pltpu.VMEM((2, 256, 256), F32),
            pltpu.VMEM(block, F32),
            pltpu.VMEM(block, F32),
            pltpu.VMEM(block, F32),
            pltpu.VMEM(block, F32),
            pltpu.VMEM(block, F32),
            pltpu.VMEM((2, 2) + block, F32),
            pltpu.VMEM((2, 2, 4, 2, 16, 128), F32),
            pltpu.VMEM((2, 2, 4, 2, 16, 128), F32),
            pltpu.VMEM((2, 4, 2, 16, 128), F32),
            pltpu.VMEM((2, 4, 2, 16, 128), F32),
            pltpu.VMEM((2, 4) + block, F32),
            pltpu.VMEM((2, 4) + block, F32),
            pltpu.VMEM((2, 1024, 256), BF16),
            pltpu.VMEM((2, 4, TAPS * 16, 1024), BF16),
            pltpu.VMEM((2,) + block, F32),
            pltpu.VMEM((2,) + block, F32),
            pltpu.VMEM(block, F32),
            pltpu.VMEM(block, F32),
            pltpu.VMEM((2, 4, ROWS, 128), F32),
            pltpu.VMEM((2, 4, ROWS, 128), F32),
            pltpu.VMEM((2, ROWS, 128), F32),
            pltpu.VMEM((4, 2, 56, 128), F32),
            pltpu.VMEM((4, 2, 56, 128), F32),
            pltpu.VMEM((4, 2, 56, 128), F32),
            pltpu.VMEM((2, 56, 128), F32),
            dma((5,)),
            dma((4,)), dma((4,)),
            dma((4,)), dma((4,)),
            dma((2, 7)), dma((2, 7)),
            dma((2, 7)), dma((2, 7)),
            dma((2, 2)), dma((2, 2)),
            dma((2, 4)), dma((2, 4)),
            dma((4,)), dma((4,)),
            dma((4,)), dma((4,)),
        ],
        compiler_params=pltpu.CompilerParams(
            collective_id=1, has_side_effects=True, vmem_limit_bytes=56 << 20
        ),
        name="backward",
    )(
        inputs.reshape(block),
        pre_gelu.reshape(block),
        output_grad.reshape(block),
        first_weight,
        second_weight,
    )
    return grad.reshape(shape), first.reshape(TAPS, 8, 128), second.reshape(TAPS, 8, 128)


def solution(mesh):
    field = P("sample", "depth", None, None, "filter")
    return jax.shard_map(
        local,
        mesh=mesh,
        in_specs=(field, field, field, P(None, None, "filter"), P(None, None, "filter")),
        out_specs=(field, P(None, "depth", "filter"), P(None, "depth", "filter")),
        check_vma=False,
    )
```

time: 257 us -> 58.7 us (0.23)
  waiting for transfers between devices: 85.5 us -> 0 us
  starting transfers between devices: 56.2 us -> 0 us
  Pallas kernels: 0 us -> 52.6 us
  local copies, waits for them, and re-layouts: 45 us -> 4.57 us
  blocking collectives: 30.8 us -> 0 us
  other arithmetic: 18.1 us -> 0 us
  matrix products: 16.9 us -> 0 us
    all_to_all x6 -> x0, waiting for transfers between devices: 83.9 us -> none  [the longest x2 75.3 us: sum_by_axis(): return jnp.sum(lax.all_to_all(own, far, 0, 0, tiled=True), axis=0)]
    pallas_call x0 -> x1, Pallas kernels: none -> 52.6 us  [local(): pl.pallas_call(kernel, out_shape=(jax.ShapeDtypeStruct(block, F32), jax.S...]
    all_to_all x6 -> x0, starting transfers between devices: 31.2 us -> none  [the longest x2 12.1 us: sum_by_axis(): return jnp.sum(lax.all_to_all(own, far, 0, 0, tiled=True), axis=0)]
    all_to_all x3 -> x0, blocking collectives: 30.8 us -> none  [summed_on_arrival(): tiles = lax.all_to_all(cut_along(array, dim, peers), axis, 0, 0, tiled=True)]
    ppermute x6 -> x0, starting transfers between devices: 25.1 us -> none  [the longest x3 19.2 us: padded_2(): lax.ppermute(head, axis, [((i + 1) % count, i) for i in range(ends)])]
    unnamed x172 -> x3, local copies, waits for them, and re-layouts: 23.1 us -> 4.57 us
    dot_general x4 -> x0, matrix products: 16.9 us -> none  [the longest x2 9.23 us: spread_back(): jnp.einsum('rtc,tic->ri', columns, kernel, precision=highest)]
    reduce_sum x8 -> x0, other arithmetic: 12.2 us -> none  [the longest x4 4.84 us: summed_on_arrival(): return jnp.sum(tiles, axis=0)]
  transfers between devices with their start and end apart: 12 -> 0, of which waited for: 5 -> 0; matrix products, arithmetic and copies ran while one was open for 20% -> 0% of each run, Pallas kernels for 0% -> 0%
where the time goes in v1:
time: 58.7 us; the launch traced here: 57.8 us
  Pallas kernels  52.6 us (90%)
  local copies, waits for them, and re-layouts  4.57 us (8%)
  between operations  0.64 us (1%)
    pallas_call x1, Pallas kernels, local(): pl.pallas_call(kernel, out_shape=(jax.ShapeDtypeStruct(block, F32), jax.S...  52.6 us
    unnamed x3, local copies, waits for them, and re-layouts  4.57 us

profile of v1, /device:TPU:8, one launch (start us, length us, event | category | flops | bytes accessed | tf_op | source)
XLA Modules:
  0.0 57.8 jit_solution(11094474764919479269)
XLA Ops:
  0.6 52.6 %backward.1 = (f32[128,128]{1,0:T(8,128)}, f32[216,128]{1,0:T(8,128)}, f32[216,128]{1,0:T(8,128)}) custom-call(f32[128,128]{1,0:T(8,128)} %bitcast.8, f32[128,128]{1,0:T(8,128)} %bitcast.9, f32[128,128]{1,0:T(8,128)} %bitcast.10, f32[27,256,128]{2,1,0:T(8,128)} %w1_hbm.1, f32[27,256,128]{2,1,0:T(8,128)} %w2_hbm.1), custom_call_target="tpu_custom_call" | custom-call | tf_op jit(solution)/shard_map/backward/pallas_call | solution.py:368
  53.3 1.5 %copy.11 = f32[1,2,8,8,128]{4,3,2,1,0:T(8,128)} copy(f32[1,2,8,8,128]{4,3,2,1,0:T(8,128)} %bitcast.11) | data formatting | bytes 131072
  54.7 1.5 %copy.12 = f32[27,8,128]{2,1,0:T(8,128)} copy(f32[27,8,128]{2,1,0:T(8,128)} %bitcast.7) | data formatting | bytes 221184
  56.3 1.5 %copy.13 = f32[27,8,128]{2,1,0:T(8,128)} copy(f32[27,8,128]{2,1,0:T(8,128)} %bitcast.6) | data formatting | bytes 221184

commit v2 on v1

--- a/solution.py
+++ b/solution.py
@@ -51,11 +51,11 @@
 
 def kernel(
     inp_hbm, pre_hbm, og_hbm, w1_hbm, w2_hbm,
-    grad_out, first_out, second_out,
+    grad_out, x_all,
     og_v, pre_v, inp_v, wf, wb1, wb2, cols, acc,
-    og_halo, pg_halo, pair_pre, pair_inp, slope_v, field_t, slices, owned, low_act, high_act,
+    og_halo, pg_halo, slope_v, field_t, slices, owned, low_act, high_act,
     og_all, pg_all, rhs, lhs, part_out, part_in, pgt_v, pg_v,
-    y_out, y_in, y_sum, z_out, z_in, x_all, x_out,
+    y_out, y_in, y_sum, z_out, z_in, x_out,
     load_sem, halo_s, halo_r, pair_s, pair_r, ring_s, ring_r, slice_s, slice_r, edge_s, edge_r,
     y_s, y_r, z_s, z_r, x_s, x_r,
 ):
@@ -70,9 +70,10 @@
 
     to_filter = (d, s, 1 - f)
     group = [(0, 1)] + [(k, o) for k in (2, 1, 3) for o in (0, 1)]
-
-    def group_device(k, o):
-        return (partner if o else d, (s + k) % 4, f)
+    wide = [(k, o, 1) for k in (2, 1, 3, 0) for o in (0, 1)] + [(k, o, 0) for k, o in group]
+
+    def group_device(k, o, g=0):
+        return (partner if o else d, (s + k) % 4, (1 - f) if g else f)
 
     to_next, to_last = ((d + 1) % 32, s, f), ((d + 31) % 32, s, f)
     to_next_chip, to_last_chip = ((d + 2) % 32, s, f), ((d + 30) % 32, s, f)
@@ -94,8 +95,8 @@
         load.start()
 
     barrier = pltpu.get_barrier_semaphore()
-    friends = [to_filter, to_next, to_last, to_next_chip, to_last_chip]
-    friends += [group_device(k, o) for k, o in group]
+    friends = [to_next, to_last, to_next_chip, to_last_chip]
+    friends += [group_device(*step) for step in wide]
     friends += [to_y(k) for k in (1, 2, 3)] + [to_z(k) for k in (1, 2, 3)]
     for friend in friends:
         pl.semaphore_signal(barrier, inc=1, device_id=friend, device_id_type=pl.DeviceIdType.MESH)
@@ -154,16 +155,25 @@
     def conv_rest(wb, h):
         return fold(acc[h] + (product(wb, h, 0) + product(wb, h, 2)))
 
-    loads[0].wait()
-    og_t = og_v[...].T
-    patch(og_t, 1)
-    og_all[c, 0] = og_v[...]
     loads[1].wait()
     act_t, slope_t = gelu_pair(pre_v[...].T)
     slope_v[...] = slope_t
-    field_t[0, f] = act_t
+    field_t[0] = act_t
     loads[2].wait()
-    field_t[1, f] = inp_v[...].T
+    field_t[1] = inp_v[...].T
+    for n in range(2):
+        for core in range(2):
+            for x in range(4):
+                for hi in range(2):
+                    for e in range(2):
+                        row = hi * 8 + e * 4
+                        slices[core, x, n, row : row + 4, :] = field_t[
+                            n, pl.ds(64 * hi + 8 * core + 2 * x + e, 4, stride=16), :
+                        ]
+    owned[c, 0, f] = slices[c, s]
+    loads[0].wait()
+    og_t = og_v[...].T
+    og_all[c, 0] = og_v[...]
 
     pl.semaphore_wait(barrier, len(friends))
 
@@ -171,9 +181,15 @@
         send(og_v.at[pl.ds(64, 64)], og_halo.at[pl.ds(0, 64)], halo_s.at[0], halo_r.at[0], to_next),
         send(og_v.at[pl.ds(0, 64)], og_halo.at[pl.ds(64, 64)], halo_s.at[1], halo_r.at[1], to_last),
     ]
-    pairs = [
-        send(pre_v, pair_pre, pair_s.at[0], pair_r.at[0], to_filter),
-        send(inp_v, pair_inp, pair_s.at[1], pair_r.at[1], to_filter),
+    sliced = [
+        send(
+            slices.at[(1 - c) if o else c, (s + k) % 4],
+            owned.at[c, (4 - k) % 4, f],
+            slice_s.at[i],
+            slice_r.at[i],
+            group_device(k, o, g),
+        )
+        for i, (k, o, g) in enumerate(wide)
     ]
 
     def gather(src, dst, n):
@@ -184,99 +200,49 @@
 
     og_gather = gather(og_v, og_all, 0)
 
+    patch(og_t, 1)
     loads[3].wait()
     split_weight(0, wb2)
     conv_middle(wb2)
-    loads[4].wait()
-    split_weight(1, wb1)
 
     for copy in og_edges:
         copy.wait_recv()
     patch_edges(og_t, og_halo)
     part_out[0] = conv_rest(wb2, 1 - f)
-    act_pair = send(part_out.at[0], part_in.at[0], pair_s.at[2], pair_r.at[2], to_filter)
+    act_pair = send(part_out.at[0], part_in.at[0], pair_s.at[0], pair_r.at[0], to_filter)
     own_part = conv_rest(wb2, f)
 
-    sliced = []
-    for n, recv in ((0, pair_pre), (1, pair_inp)):
-        pairs[n].wait_recv()
-        other = recv[...].T
-        if n == 0:
-            other, _ = gelu_pair(other)
-        field_t[n, 1 - f] = other
-        for half in range(2):
-            for core in range(2):
-                for x in range(4):
-                    for hi in range(2):
-                        for e in range(2):
-                            row = hi * 8 + e * 4
-                            slices[n, core, x, half, row : row + 4, :] = field_t[
-                                n, half, pl.ds(64 * hi + 8 * core + 2 * x + e, 4, stride=16), :
-                            ]
-        owned[n, c, 0] = slices[n, c, s]
-        sliced.append(
-            [
-                send(
-                    slices.at[n, (1 - c) if o else c, (s + k) % 4],
-                    owned.at[n, c, (4 - k) % 4],
-                    slice_s.at[n, i],
-                    slice_r.at[n, i],
-                    group_device(k, o),
-                )
-                for i, (k, o) in enumerate(group)
-            ]
-        )
-    edges = []
-    for n in range(2):
-        for copy in sliced[n]:
-            copy.wait_recv()
-        edges.append(
-            [
-                send(owned.at[n, 1], low_act.at[n], edge_s.at[n, 0], edge_r.at[n, 0], to_next_chip),
-                send(owned.at[n, 0], high_act.at[n], edge_s.at[n, 1], edge_r.at[n, 1], to_last_chip),
-            ]
-        )
-
-    act_pair.wait_recv()
-    pg_t = (own_part + part_in[0]) * slope_v[...]
-    pgt_v[...] = pg_t
-    pg_v[...] = pg_t.T
-    pg_gather = gather(pg_v, pg_all, 1)
-    pg_edges = [
-        send(pg_v.at[pl.ds(64, 64)], pg_halo.at[pl.ds(0, 64)], halo_s.at[2], halo_r.at[2], to_next),
-        send(pg_v.at[pl.ds(0, 64)], pg_halo.at[pl.ds(64, 64)], halo_s.at[3], halo_r.at[3], to_last),
-    ]
-    pg_all[c, 0] = pg_v[...]
-    patch(pg_t, 1)
-    conv_middle(wb1)
+    for copy in sliced:
+        copy.wait_recv()
+    edges = [
+        send(owned.at[1], low_act, edge_s.at[0], edge_r.at[0], to_next_chip),
+        send(owned.at[0], high_act, edge_s.at[1], edge_r.at[1], to_last_chip),
+    ]
 
     def make_rhs(n, ref):
         high, low = parts_of(ref[...].reshape(1024, 128))
         rhs[n, :, 0:128] = high
         rhs[n, :, 128:256] = low
 
-    def make_lhs(n):
-        for copy in edges[n]:
-            copy.wait_recv()
+    def make_lhs(n, own_planes):
         near = lanes_of(32) < 64
 
+        def joined(one, two):
+            return pltpu.roll(jnp.where(near, two, one), 64, 1)
+
         def body(k, carry):
-            first = owned[n, 0, k].reshape(32, 128)
-            last = owned[n, 1, k].reshape(32, 128)
-            below = jnp.where(chip == 0, 0.0, low_act[n, k].reshape(32, 128))
-            above = jnp.where(chip == 15, 0.0, high_act[n, k].reshape(32, 128))
-
-            def joined(one, two):
-                return pltpu.roll(jnp.where(near, two, one), 64, 1)
-
-            middle = joined(first, last)
-            bases = [
-                (joined(below, first), ((0, 0),)),
-                (first, ((1, 0),)),
-                (middle, ((2, 0), (0, 1))),
-                (last, ((1, 1),)),
-                (joined(last, above), ((2, 1),)),
-            ]
+            first = owned[0, k, :, n].reshape(32, 128)
+            last = owned[1, k, :, n].reshape(32, 128)
+            if own_planes:
+                bases = [
+                    (first, ((1, 0),)),
+                    (joined(first, last), ((2, 0), (0, 1))),
+                    (last, ((1, 1),)),
+                ]
+            else:
+                below = jnp.where(chip == 0, 0.0, low_act[k, :, n].reshape(32, 128))
+                above = jnp.where(chip == 15, 0.0, high_act[k, :, n].reshape(32, 128))
+                bases = [(joined(below, first), ((0, 0),)), (joined(last, above), ((2, 1),))]
             for base, uses in bases:
                 for b in range(3):
                     for e in range(3):
@@ -312,9 +278,30 @@
     for copy in og_gather:
         copy.wait_recv()
     make_rhs(0, og_all)
-    make_lhs(0)
+    make_lhs(0, True)
+    make_lhs(1, True)
+
+    act_pair.wait_recv()
+    pg_t = (own_part + part_in[0]) * slope_v[...]
+    pgt_v[...] = pg_t
+    pg_v[...] = pg_t.T
+    pg_gather = gather(pg_v, pg_all, 1)
+    pg_edges = [
+        send(pg_v.at[pl.ds(64, 64)], pg_halo.at[pl.ds(0, 64)], halo_s.at[2], halo_r.at[2], to_next),
+        send(pg_v.at[pl.ds(0, 64)], pg_halo.at[pl.ds(64, 64)], halo_s.at[3], halo_r.at[3], to_last),
+    ]
+    pg_all[c, 0] = pg_v[...]
+
+    patch(pg_t, 1)
+    loads[4].wait()
+    split_weight(1, wb1)
+    conv_middle(wb1)
+
+    for copy in edges:
+        copy.wait_recv()
+    make_lhs(0, False)
     second_y = raw(0)
-    make_lhs(1)
+    make_lhs(1, False)
     for copy in pg_gather:
         copy.wait_recv()
     make_rhs(1, pg_all)
@@ -324,7 +311,7 @@
         copy.wait_recv()
     patch_edges(pgt_v[...], pg_halo)
     part_out[1] = conv_rest(wb1, 1 - f)
-    in_pair = send(part_out.at[1], part_in.at[1], pair_s.at[3], pair_r.at[3], to_filter)
+    in_pair = send(part_out.at[1], part_in.at[1], pair_s.at[1], pair_r.at[1], to_filter)
     own_grad = conv_rest(wb1, f)
 
     for n, copies in ((0, second_y), (1, first_y)):
@@ -346,17 +333,21 @@
     x_all[s] = x_out[...]
 
     in_pair.wait_recv()
-    grad_out[...] = (own_grad + part_in[1]).T
+    grad_out[...] = own_grad + part_in[1]
 
     for copy in x_copies:
         copy.wait_recv()
+
+    for copy in started:
+        copy.wait_send()
+
+
+def finish(grad_t, x_all, grad_out, first_out, second_out):
+    grad_out[...] = grad_t[...].T
     for n, out in ((0, second_out), (1, first_out)):
         for x in range(4):
             for e in range(2):
                 out[pl.ds(2 * x + e, TAPS, stride=8), :] = x_all[x, n, pl.ds(e, TAPS, stride=2), :]
-
-    for copy in started:
-        copy.wait_send()
 
 
 def local(inputs, pre_gelu, output_grad, first_weight, second_weight):
@@ -365,15 +356,14 @@
     vmem = pl.BlockSpec(memory_space=pltpu.VMEM)
     dma = pltpu.SemaphoreType.DMA
     block = (128, 128)
-    grad, first, second = pl.pallas_call(
+    parts = pl.pallas_call(
         kernel,
         out_shape=(
             jax.ShapeDtypeStruct(block, F32),
-            jax.ShapeDtypeStruct((ROWS, 128), F32),
-            jax.ShapeDtypeStruct((ROWS, 128), F32),
+            jax.ShapeDtypeStruct((4, 2, 56, 128), F32),
         ),
         in_specs=[hbm] * 5,
-        out_specs=(vmem, vmem, vmem),
+        out_specs=(vmem, vmem),
         scratch_shapes=[
             pltpu.VMEM(block, F32),
             pltpu.VMEM(block, F32),
@@ -386,13 +376,11 @@
             pltpu.VMEM(block, F32),
             pltpu.VMEM(block, F32),
             pltpu.VMEM(block, F32),
-            pltpu.VMEM(block, F32),
-            pltpu.VMEM(block, F32),
-            pltpu.VMEM((2, 2) + block, F32),
-            pltpu.VMEM((2, 2, 4, 2, 16, 128), F32),
-            pltpu.VMEM((2, 2, 4, 2, 16, 128), F32),
+            pltpu.VMEM((2,) + block, F32),
             pltpu.VMEM((2, 4, 2, 16, 128), F32),
-            pltpu.VMEM((2, 4, 2, 16, 128), F32),
+            pltpu.VMEM((2, 4, 2, 2, 16, 128), F32),
+            pltpu.VMEM((4, 2, 2, 16, 128), F32),
+            pltpu.VMEM((4, 2, 2, 16, 128), F32),
             pltpu.VMEM((2, 4) + block, F32),
             pltpu.VMEM((2, 4) + block, F32),
             pltpu.VMEM((2, 1024, 256), BF16),
@@ -406,14 +394,13 @@
             pltpu.VMEM((2, ROWS, 128), F32),
             pltpu.VMEM((4, 2, 56, 128), F32),
             pltpu.VMEM((4, 2, 56, 128), F32),
-            pltpu.VMEM((4, 2, 56, 128), F32),
             pltpu.VMEM((2, 56, 128), F32),
             dma((5,)),
             dma((4,)), dma((4,)),
-            dma((4,)), dma((4,)),
+            dma((2,)), dma((2,)),
             dma((2, 7)), dma((2, 7)),
-            dma((2, 7)), dma((2, 7)),
-            dma((2, 2)), dma((2, 2)),
+            dma((15,)), dma((15,)),
+            dma((2,)), dma((2,)),
             dma((2, 4)), dma((2, 4)),
             dma((4,)), dma((4,)),
             dma((4,)), dma((4,)),
@@ -429,6 +416,17 @@
         first_weight,
         second_weight,
     )
+    grad, first, second = pl.pallas_call(
+        finish,
+        out_shape=(
+            jax.ShapeDtypeStruct(block, F32),
+            jax.ShapeDtypeStruct((ROWS, 128), F32),
+            jax.ShapeDtypeStruct((ROWS, 128), F32),
+        ),
+        in_specs=[vmem] * 2,
+        out_specs=(vmem, vmem, vmem),
+        name="finish",
+    )(*parts)
     return grad.reshape(shape), first.reshape(TAPS, 8, 128), second.reshape(TAPS, 8, 128)
 
 

time: 58.7 us -> 55.9 us (0.952)
  local copies, waits for them, and re-layouts: 4.57 us -> 0 us
  Pallas kernels: 52.6 us -> 54.5 us
    unnamed x3 -> x0, local copies, waits for them, and re-layouts: 4.57 us -> none
    pallas_call x0 -> x1, Pallas kernels: none -> 1.71 us  [local(): pl.pallas_call(finish, out_shape=(jax.ShapeDtypeStruct(block, F32), jax.S...]
where the time goes in v2:
time: 55.9 us; the launch traced here: 55.2 us
  Pallas kernels  54.5 us (97%)
  between operations  0.64 us (1%)
    pallas_call x1, Pallas kernels, local(): pl.pallas_call(kernel, out_shape=(jax.ShapeDtypeStruct(block, F32), jax.S...  52.8 us
    pallas_call x1, Pallas kernels, local(): pl.pallas_call(finish, out_shape=(jax.ShapeDtypeStruct(block, F32), jax.S...  1.71 us

profile of v2, /device:TPU:8, one launch (start us, length us, event | category | flops | bytes accessed | tf_op | source)
XLA Modules:
  0.0 55.2 jit_solution(1881465013316758725)
XLA Ops:
  0.6 52.8 %backward.1 = (f32[128,128]{1,0:T(8,128)}, f32[4,2,56,128]{3,2,1,0:T(8,128)}) custom-call(f32[128,128]{1,0:T(8,128)} %bitcast.6, f32[128,128]{1,0:T(8,128)} %bitcast.7, f32[128,128]{1,0:T(8,128)} %bitcast.8, f32[27,256,128]{2,1,0:T(8,128)} %w1_hbm.1, f32[27,256,128]{2,1,0:T(8,128)} %w2_hbm.1), custom_call_target="tpu_custom_call" | custom-call | tf_op jit(solution)/shard_map/backward/pallas_call | solution.py:359
  53.5 1.7 %finish.1 = (f32[128,128]{1,0:T(8,128)}, f32[216,128]{1,0:T(8,128)}, f32[216,128]{1,0:T(8,128)}) custom-call(f32[128,128]{1,0:T(8,128)} %get-tuple-element.8.grad_t, f32[4,2,56,128]{3,2,1,0:T(8,128)} %get-tuple-element.9.x_all), custom_call_target="tpu_custom_call" | custom-call | tf_op jit(solution)/shard_map/finish/pallas_call | solution.py:419

commit v3 on v2

--- a/solution.py
+++ b/solution.py
@@ -53,10 +53,10 @@
     inp_hbm, pre_hbm, og_hbm, w1_hbm, w2_hbm,
     grad_out, x_all,
     og_v, pre_v, inp_v, wf, wb1, wb2, cols, acc,
-    og_halo, pg_halo, slope_v, field_t, slices, owned, low_act, high_act,
+    og_halo, pg_halo, pair_pre, pair_inp, slope_v, field_t, slices, owned, edge_out, edge_in,
     og_all, pg_all, rhs, lhs, part_out, part_in, pgt_v, pg_v,
     y_out, y_in, y_sum, z_out, z_in, x_out,
-    load_sem, halo_s, halo_r, pair_s, pair_r, ring_s, ring_r, slice_s, slice_r, edge_s, edge_r,
+    load_sem, halo_s, halo_r, pair_s, pair_r, field_s, field_r, ring_s, ring_r, slice_s, slice_r, edge_s, edge_r,
     y_s, y_r, z_s, z_r, x_s, x_r,
 ):
     d = lax.axis_index("depth")
@@ -70,10 +70,9 @@
 
     to_filter = (d, s, 1 - f)
     group = [(0, 1)] + [(k, o) for k in (2, 1, 3) for o in (0, 1)]
-    wide = [(k, o, 1) for k in (2, 1, 3, 0) for o in (0, 1)] + [(k, o, 0) for k, o in group]
-
-    def group_device(k, o, g=0):
-        return (partner if o else d, (s + k) % 4, (1 - f) if g else f)
+
+    def group_device(k, o):
+        return (partner if o else d, (s + k) % 4, f)
 
     to_next, to_last = ((d + 1) % 32, s, f), ((d + 31) % 32, s, f)
     to_next_chip, to_last_chip = ((d + 2) % 32, s, f), ((d + 30) % 32, s, f)
@@ -95,8 +94,8 @@
         load.start()
 
     barrier = pltpu.get_barrier_semaphore()
-    friends = [to_next, to_last, to_next_chip, to_last_chip]
-    friends += [group_device(*step) for step in wide]
+    friends = [to_filter, to_next, to_last, to_next_chip, to_last_chip]
+    friends += [group_device(k, o) for k, o in group]
     friends += [to_y(k) for k in (1, 2, 3)] + [to_z(k) for k in (1, 2, 3)]
     for friend in friends:
         pl.semaphore_signal(barrier, inc=1, device_id=friend, device_id_type=pl.DeviceIdType.MESH)
@@ -155,25 +154,28 @@
     def conv_rest(wb, h):
         return fold(acc[h] + (product(wb, h, 0) + product(wb, h, 2)))
 
-    loads[1].wait()
-    act_t, slope_t = gelu_pair(pre_v[...].T)
-    slope_v[...] = slope_t
-    field_t[0] = act_t
-    loads[2].wait()
-    field_t[1] = inp_v[...].T
-    for n in range(2):
+    def slice_field(n, half):
         for core in range(2):
             for x in range(4):
                 for hi in range(2):
                     for e in range(2):
                         row = hi * 8 + e * 4
-                        slices[core, x, n, row : row + 4, :] = field_t[
-                            n, pl.ds(64 * hi + 8 * core + 2 * x + e, 4, stride=16), :
+                        slices[n, core, x, half, row : row + 4, :] = field_t[
+                            n, half, pl.ds(64 * hi + 8 * core + 2 * x + e, 4, stride=16), :
                         ]
-    owned[c, 0, f] = slices[c, s]
+
     loads[0].wait()
     og_t = og_v[...].T
+    patch(og_t, 1)
     og_all[c, 0] = og_v[...]
+    loads[1].wait()
+    act_t, slope_t = gelu_pair(pre_v[...].T)
+    slope_v[...] = slope_t
+    field_t[0, f] = act_t
+    slice_field(0, f)
+    loads[2].wait()
+    field_t[1, f] = inp_v[...].T
+    slice_field(1, f)
 
     pl.semaphore_wait(barrier, len(friends))
 
@@ -181,26 +183,30 @@
         send(og_v.at[pl.ds(64, 64)], og_halo.at[pl.ds(0, 64)], halo_s.at[0], halo_r.at[0], to_next),
         send(og_v.at[pl.ds(0, 64)], og_halo.at[pl.ds(64, 64)], halo_s.at[1], halo_r.at[1], to_last),
     ]
-    sliced = [
-        send(
-            slices.at[(1 - c) if o else c, (s + k) % 4],
-            owned.at[c, (4 - k) % 4, f],
-            slice_s.at[i],
-            slice_r.at[i],
-            group_device(k, o, g),
-        )
-        for i, (k, o, g) in enumerate(wide)
-    ]
+    pre_pair = send(pre_v, pair_pre, field_s.at[0], field_r.at[0], to_filter)
 
     def gather(src, dst, n):
-        return [
-            send(src, dst.at[c, (4 - k) % 4], ring_s.at[n, i], ring_r.at[n, i], group_device(k, o))
-            for i, (k, o) in enumerate(group)
-        ]
+        copies = [send(src, dst.at[c, 0], ring_s.at[n, 0], ring_r.at[n, 0], group_device(0, 1))]
+        for k in (2, 1, 3):
+            copies.append(
+                send(src, dst.at[c, 4 - k], ring_s.at[n, k], ring_r.at[n, k], group_device(k, 0))
+            )
+        return copies
+
+    def gather_on(copies, dst, n):
+        passed = [copies[0]]
+        for k, copy in ((1, copies[2]), (3, copies[3]), (2, copies[1])):
+            j = 4 - k
+            copy.wait_recv()
+            passed.append(
+                send(
+                    dst.at[c, j], dst.at[c, j], ring_s.at[n, 3 + j], ring_r.at[n, 3 + j], group_device(0, 1)
+                )
+            )
+        return passed
 
     og_gather = gather(og_v, og_all, 0)
 
-    patch(og_t, 1)
     loads[3].wait()
     split_weight(0, wb2)
     conv_middle(wb2)
@@ -210,14 +216,40 @@
     patch_edges(og_t, og_halo)
     part_out[0] = conv_rest(wb2, 1 - f)
     act_pair = send(part_out.at[0], part_in.at[0], pair_s.at[0], pair_r.at[0], to_filter)
+    inp_pair = send(inp_v, pair_inp, field_s.at[1], field_r.at[1], to_filter)
     own_part = conv_rest(wb2, f)
 
-    for copy in sliced:
-        copy.wait_recv()
-    edges = [
-        send(owned.at[1], low_act, edge_s.at[0], edge_r.at[0], to_next_chip),
-        send(owned.at[0], high_act, edge_s.at[1], edge_r.at[1], to_last_chip),
-    ]
+    def send_slices(n, pair, recv):
+        pair.wait_recv()
+        other = recv[...].T
+        if n == 0:
+            other, _ = gelu_pair(other)
+        field_t[n, 1 - f] = other
+        slice_field(n, 1 - f)
+        owned[n, c, 0] = slices[n, c, s]
+        return [
+            send(
+                slices.at[n, (1 - c) if o else c, (s + k) % 4],
+                owned.at[n, c, (4 - k) % 4],
+                slice_s.at[n, i],
+                slice_r.at[n, i],
+                group_device(k, o),
+            )
+            for i, (k, o) in enumerate(group)
+        ]
+
+    near_edge = lax.broadcasted_iota(jnp.int32, (4, 16, 128), 2) < 64
+
+    def send_edges(n, copies):
+        for copy in copies:
+            copy.wait_recv()
+        above, below = owned[n, 1], owned[n, 0]
+        edge_out[n, 0] = jnp.where(near_edge, pltpu.roll(above[:, 0], 64, 2), above[:, 1])
+        edge_out[n, 1] = jnp.where(near_edge, below[:, 0], pltpu.roll(below[:, 1], 64, 2))
+        return [
+            send(edge_out.at[n, i], edge_in.at[n, i], edge_s.at[n, i], edge_r.at[n, i], device)
+            for i, device in enumerate((to_next_chip, to_last_chip))
+        ]
 
     def make_rhs(n, ref):
         high, low = parts_of(ref[...].reshape(1024, 128))
@@ -231,8 +263,8 @@
             return pltpu.roll(jnp.where(near, two, one), 64, 1)
 
         def body(k, carry):
-            first = owned[0, k, :, n].reshape(32, 128)
-            last = owned[1, k, :, n].reshape(32, 128)
+            first = owned[n, 0, k].reshape(32, 128)
+            last = owned[n, 1, k].reshape(32, 128)
             if own_planes:
                 bases = [
                     (first, ((1, 0),)),
@@ -240,8 +272,11 @@
                     (last, ((1, 1),)),
                 ]
             else:
-                below = jnp.where(chip == 0, 0.0, low_act[k, :, n].reshape(32, 128))
-                above = jnp.where(chip == 15, 0.0, high_act[k, :, n].reshape(32, 128))
+                below, above = edge_in[n, 0, k], edge_in[n, 1, k]
+                below = jnp.concatenate([pltpu.roll(below, 64, 1), below], axis=0)
+                above = jnp.concatenate([above, pltpu.roll(above, 64, 1)], axis=0)
+                below = jnp.where(chip == 0, 0.0, below)
+                above = jnp.where(chip == 15, 0.0, above)
                 bases = [(joined(below, first), ((0, 0),)), (joined(last, above), ((2, 1),))]
             for base, uses in bases:
                 for b in range(3):
@@ -275,11 +310,13 @@
         y_sum[n] = raw_chunk(n, 0)
         return copies
 
-    for copy in og_gather:
+    loads[4].wait()
+    split_weight(1, wb1)
+    og_passed = gather_on(og_gather, og_all, 0)
+    act_slices = send_slices(0, pre_pair, pair_pre)
+    for copy in og_passed:
         copy.wait_recv()
     make_rhs(0, og_all)
-    make_lhs(0, True)
-    make_lhs(1, True)
 
     act_pair.wait_recv()
     pg_t = (own_part + part_in[0]) * slope_v[...]
@@ -292,20 +329,19 @@
     ]
     pg_all[c, 0] = pg_v[...]
 
+    act_edges = send_edges(0, act_slices)
+    inp_slices = send_slices(1, inp_pair, pair_inp)
+    make_lhs(0, True)
     patch(pg_t, 1)
-    loads[4].wait()
-    split_weight(1, wb1)
     conv_middle(wb1)
 
-    for copy in edges:
+    for copy in act_edges:
         copy.wait_recv()
     make_lhs(0, False)
     second_y = raw(0)
-    make_lhs(1, False)
-    for copy in pg_gather:
-        copy.wait_recv()
-    make_rhs(1, pg_all)
-    first_y = raw(1)
+    inp_edges = send_edges(1, inp_slices)
+    make_lhs(1, True)
+    pg_passed = gather_on(pg_gather, pg_all, 1)
 
     for copy in pg_edges:
         copy.wait_recv()
@@ -314,28 +350,44 @@
     in_pair = send(part_out.at[1], part_in.at[1], pair_s.at[1], pair_r.at[1], to_filter)
     own_grad = conv_rest(wb1, f)
 
-    for n, copies in ((0, second_y), (1, first_y)):
+    for copy in inp_edges:
+        copy.wait_recv()
+    make_lhs(1, False)
+    for copy in pg_passed:
+        copy.wait_recv()
+    make_rhs(1, pg_all)
+    first_y = raw(1)
+
+    def sum_y(n, copies):
         for copy in copies:
             copy.wait_recv()
         y_sum[n] = (y_sum[n] + y_in[n, 1]) + (y_in[n, 2] + y_in[n, 3])
         for zz in range(4):
-            z_out[zz, n, 0:54, :] = y_sum[n, pl.ds(zz, 54, stride=4), :]
-            z_out[zz, n, 54:56, :] = jnp.zeros((2, 128), F32)
-    z_copies = [
-        send(z_out.at[(zl + k) % 4], z_in.at[4 - k], z_s.at[k], z_r.at[k], to_z(k)) for k in (1, 2, 3)
-    ]
-    for copy in z_copies:
-        copy.wait_recv()
-    x_out[...] = ((z_out[zl] + z_in[1]) + (z_in[2] + z_in[3])) * (1.0 / 128.0)
-    x_copies = [
-        send(x_out, x_all.at[s], x_s.at[k], x_r.at[k], (d, (s + k) % 4, f)) for k in (1, 2, 3)
-    ]
-    x_all[s] = x_out[...]
-
+            z_out[n, zz, 0:54, :] = y_sum[n, pl.ds(zz, 54, stride=4), :]
+            z_out[n, zz, 54:56, :] = jnp.zeros((2, 128), F32)
+        return [
+            send(z_out.at[n, (zl + k) % 4], z_in.at[n, 4 - k], z_s.at[n, k], z_r.at[n, k], to_z(k))
+            for k in (2, 1, 3)
+        ]
+
+    def sum_z(n, copies):
+        for copy in copies:
+            copy.wait_recv()
+        total = (z_out[n, zl] + z_in[n, 1]) + (z_in[n, 2] + z_in[n, 3])
+        x_out[n] = total * (1.0 / 128.0)
+        x_all[n, s] = x_out[n]
+        return [
+            send(x_out.at[n], x_all.at[n, s], x_s.at[n, k], x_r.at[n, k], group_device(k, 0))
+            for k in (2, 1, 3)
+        ]
+
+    second_z = sum_y(0, second_y)
+    first_z = sum_y(1, first_y)
+    second_x = sum_z(0, second_z)
     in_pair.wait_recv()
     grad_out[...] = own_grad + part_in[1]
-
-    for copy in x_copies:
+    first_x = sum_z(1, first_z)
+    for copy in second_x + first_x:
         copy.wait_recv()
 
     for copy in started:
@@ -347,7 +399,7 @@
     for n, out in ((0, second_out), (1, first_out)):
         for x in range(4):
             for e in range(2):
-                out[pl.ds(2 * x + e, TAPS, stride=8), :] = x_all[x, n, pl.ds(e, TAPS, stride=2), :]
+                out[pl.ds(2 * x + e, TAPS, stride=8), :] = x_all[n, x, pl.ds(e, TAPS, stride=2), :]
 
 
 def local(inputs, pre_gelu, output_grad, first_weight, second_weight):
@@ -360,7 +412,7 @@
         kernel,
         out_shape=(
             jax.ShapeDtypeStruct(block, F32),
-            jax.ShapeDtypeStruct((4, 2, 56, 128), F32),
+            jax.ShapeDtypeStruct((2, 4, 56, 128), F32),
         ),
         in_specs=[hbm] * 5,
         out_specs=(vmem, vmem),
@@ -376,11 +428,13 @@
             pltpu.VMEM(block, F32),
             pltpu.VMEM(block, F32),
             pltpu.VMEM(block, F32),
-            pltpu.VMEM((2,) + block, F32),
-            pltpu.VMEM((2, 4, 2, 16, 128), F32),
-            pltpu.VMEM((2, 4, 2, 2, 16, 128), F32),
-            pltpu.VMEM((4, 2, 2, 16, 128), F32),
-            pltpu.VMEM((4, 2, 2, 16, 128), F32),
+            pltpu.VMEM(block, F32),
+            pltpu.VMEM(block, F32),
+            pltpu.VMEM((2, 2) + block, F32),
+            pltpu.VMEM((2, 2, 4, 2, 16, 128), F32),
+            pltpu.VMEM((2, 2, 4, 2, 16, 128), F32),
+            pltpu.VMEM((2, 2, 4, 16, 128), F32),
+            pltpu.VMEM((2, 2, 4, 16, 128), F32),
             pltpu.VMEM((2, 4) + block, F32),
             pltpu.VMEM((2, 4) + block, F32),
             pltpu.VMEM((2, 1024, 256), BF16),
@@ -392,18 +446,19 @@
             pltpu.VMEM((2, 4, ROWS, 128), F32),
             pltpu.VMEM((2, 4, ROWS, 128), F32),
             pltpu.VMEM((2, ROWS, 128), F32),
-            pltpu.VMEM((4, 2, 56, 128), F32),
-            pltpu.VMEM((4, 2, 56, 128), F32),
+            pltpu.VMEM((2, 4, 56, 128), F32),
+            pltpu.VMEM((2, 4, 56, 128), F32),
             pltpu.VMEM((2, 56, 128), F32),
             dma((5,)),
             dma((4,)), dma((4,)),
             dma((2,)), dma((2,)),
+            dma((2,)), dma((2,)),
             dma((2, 7)), dma((2, 7)),
-            dma((15,)), dma((15,)),
-            dma((2,)), dma((2,)),
+            dma((2, 7)), dma((2, 7)),
+            dma((2, 2)), dma((2, 2)),
             dma((2, 4)), dma((2, 4)),
-            dma((4,)), dma((4,)),
-            dma((4,)), dma((4,)),
+            dma((2, 4)), dma((2, 4)),
+            dma((2, 4)), dma((2, 4)),
         ],
         compiler_params=pltpu.CompilerParams(
             collective_id=1, has_side_effects=True, vmem_limit_bytes=56 << 20

time: 55.9 us -> 54.5 us (0.975)
  Pallas kernels: 54.5 us -> 53.2 us
    pallas_call x1, Pallas kernels: 52.8 us -> 51.5 us  [local(): pl.pallas_call(kernel, out_shape=(jax.ShapeDtypeStruct(block, F32), jax.S...]
where the time goes in v3:
time: 54.5 us; the launch traced here: 53.8 us
  Pallas kernels  53.2 us (98%)
  between operations  0.64 us (1%)
    pallas_call x1, Pallas kernels, local(): pl.pallas_call(kernel, out_shape=(jax.ShapeDtypeStruct(block, F32), jax.S...  51.5 us
    pallas_call x1, Pallas kernels, local(): pl.pallas_call(finish, out_shape=(jax.ShapeDtypeStruct(block, F32), jax.S...  1.71 us

profile of v3, /device:TPU:8, one launch (start us, length us, event | category | flops | bytes accessed | tf_op | source)
XLA Modules:
  0.0 53.8 jit_solution(10892705200149333096)
XLA Ops:
  0.6 51.5 %backward.1 = (f32[128,128]{1,0:T(8,128)}, f32[2,4,56,128]{3,2,1,0:T(8,128)}) custom-call(f32[128,128]{1,0:T(8,128)} %bitcast.6, f32[128,128]{1,0:T(8,128)} %bitcast.7, f32[128,128]{1,0:T(8,128)} %bitcast.8, f32[27,256,128]{2,1,0:T(8,128)} %w1_hbm.1, f32[27,256,128]{2,1,0:T(8,128)} %w2_hbm.1), custom_call_target="tpu_custom_call" | custom-call | tf_op jit(solution)/shard_map/backward/pallas_call | solution.py:411
  52.1 1.7 %finish.1 = (f32[128,128]{1,0:T(8,128)}, f32[216,128]{1,0:T(8,128)}, f32[216,128]{1,0:T(8,128)}) custom-call(f32[128,128]{1,0:T(8,128)} %get-tuple-element.8.grad_t, f32[2,4,56,128]{3,2,1,0:T(8,128)} %get-tuple-element.9.x_all), custom_call_target="tpu_custom_call" | custom-call | tf_op jit(solution)/shard_map/finish/pallas_call | solution.py:474

commit v4 on v3

--- a/solution.py
+++ b/solution.py
@@ -53,10 +53,10 @@
     inp_hbm, pre_hbm, og_hbm, w1_hbm, w2_hbm,
     grad_out, x_all,
     og_v, pre_v, inp_v, wf, wb1, wb2, cols, acc,
-    og_halo, pg_halo, pair_pre, pair_inp, slope_v, field_t, slices, owned, edge_out, edge_in,
-    og_all, pg_all, rhs, lhs, part_out, part_in, pgt_v, pg_v,
+    og_halo, pg_halo, pair_in, slope_v, field_t, slices, owned, edge_out, edge_in,
+    og_all, pg_all, rhs_og, rhs_pg, lhs_act, lhs_inp, part_out, part_in, pgt_v, pg_v,
     y_out, y_in, y_sum, z_out, z_in, x_out,
-    load_sem, halo_s, halo_r, pair_s, pair_r, field_s, field_r, ring_s, ring_r, slice_s, slice_r, edge_s, edge_r,
+    load_sem, halo_s, halo_r, pair_s, pair_r, field_s, field_r, ring_s, ring_r, rim_s, rim_r, slice_s, slice_r, edge_s, edge_r,
     y_s, y_r, z_s, z_r, x_s, x_r,
 ):
     d = lax.axis_index("depth")
@@ -120,7 +120,7 @@
                 cols[t * 128 : (t + 1) * 128, 128:256] = low
 
     def patch_edges(own, halo_ref):
-        edge = halo_ref[...].T
+        edge = halo_ref[...].reshape(128, 128).T
         edge = jnp.where(left & (d == 0), 0.0, edge)
         edge = jnp.where((~left) & (d == 31), 0.0, edge)
         swapped = pltpu.roll(own, 64, 1)
@@ -154,42 +154,73 @@
     def conv_rest(wb, h):
         return fold(acc[h] + (product(wb, h, 0) + product(wb, h, 2)))
 
-    def slice_field(n, half):
+    def slice_field(n, value):
+        field_t[n] = value
         for core in range(2):
             for x in range(4):
                 for hi in range(2):
                     for e in range(2):
                         row = hi * 8 + e * 4
-                        slices[n, core, x, half, row : row + 4, :] = field_t[
-                            n, half, pl.ds(64 * hi + 8 * core + 2 * x + e, 4, stride=16), :
+                        slices[n, core, x, row : row + 4, :] = field_t[
+                            n, pl.ds(64 * hi + 8 * core + 2 * x + e, 4, stride=16), :
                         ]
+        owned[n, c, 0, f] = slices[n, c, s]
 
     loads[0].wait()
-    og_t = og_v[...].T
+    og_t = og_v[...].reshape(128, 128).T
     patch(og_t, 1)
-    og_all[c, 0] = og_v[...]
+    og_all[0, pl.ds(1 + 2 * c, 2)] = og_v[...]
     loads[1].wait()
     act_t, slope_t = gelu_pair(pre_v[...].T)
     slope_v[...] = slope_t
-    field_t[0, f] = act_t
-    slice_field(0, f)
+    slice_field(0, act_t)
     loads[2].wait()
-    field_t[1, f] = inp_v[...].T
-    slice_field(1, f)
+    slice_field(1, inp_v[...].T)
+
+    def clear(k, carry):
+        for yy in range(4):
+            for t, n in ((0, 0), (18, 2)):
+                at = pl.ds(pl.multiple_of(k * 384 + n * 128, 128), 128)
+                lhs_act[yy, t * 16 : (t + 9) * 16, at] = jnp.zeros((144, 128), BF16)
+        return carry
+
+    lax.fori_loop(0, 4, clear, 0)
 
     pl.semaphore_wait(barrier, len(friends))
 
     og_edges = [
-        send(og_v.at[pl.ds(64, 64)], og_halo.at[pl.ds(0, 64)], halo_s.at[0], halo_r.at[0], to_next),
-        send(og_v.at[pl.ds(0, 64)], og_halo.at[pl.ds(64, 64)], halo_s.at[1], halo_r.at[1], to_last),
+        send(og_v.at[1], og_halo.at[0], halo_s.at[0], halo_r.at[0], to_next),
+        send(og_v.at[0], og_halo.at[1], halo_s.at[1], halo_r.at[1], to_last),
     ]
-    pre_pair = send(pre_v, pair_pre, field_s.at[0], field_r.at[0], to_filter)
+    field_pairs = [
+        send(slices.at[n], pair_in.at[n], field_s.at[n], field_r.at[n], to_filter) for n in (1, 0)
+    ][::-1]
+
+    def send_slices(n, kind, src, half):
+        return [
+            send(
+                src.at[n, (1 - c) if o else c, (s + k) % 4],
+                owned.at[n, c, (4 - k) % 4, half],
+                slice_s.at[n, kind, i],
+                slice_r.at[n, kind, i],
+                group_device(k, o),
+            )
+            for i, (k, o) in enumerate(group)
+        ]
+
+    slice_copies = [send_slices(n, 0, slices, f) for n in (1, 0)][::-1]
+
+    def pass_slices(n):
+        field_pairs[n].wait_recv()
+        owned[n, c, 0, 1 - f] = pair_in[n, c, s]
+        slice_copies[n] += send_slices(n, 1, pair_in, 1 - f)
+
 
     def gather(src, dst, n):
-        copies = [send(src, dst.at[c, 0], ring_s.at[n, 0], ring_r.at[n, 0], group_device(0, 1))]
+        copies = [send(src, dst(0), ring_s.at[n, 0], ring_r.at[n, 0], group_device(0, 1))]
         for k in (2, 1, 3):
             copies.append(
-                send(src, dst.at[c, 4 - k], ring_s.at[n, k], ring_r.at[n, k], group_device(k, 0))
+                send(src, dst(4 - k), ring_s.at[n, k], ring_r.at[n, k], group_device(k, 0))
             )
         return copies
 
@@ -200,12 +231,18 @@
             copy.wait_recv()
             passed.append(
                 send(
-                    dst.at[c, j], dst.at[c, j], ring_s.at[n, 3 + j], ring_r.at[n, 3 + j], group_device(0, 1)
+                    dst(j), dst(j), ring_s.at[n, 3 + j], ring_r.at[n, 3 + j], group_device(0, 1)
                 )
             )
         return passed
 
-    og_gather = gather(og_v, og_all, 0)
+    def og_planes(slot):
+        return og_all.at[slot, pl.ds(1 + 2 * c, 2)]
+
+    def pg_planes(slot):
+        return pg_all.at[c, slot]
+
+    og_gather = gather(og_v, og_planes, 0)
 
     loads[3].wait()
     split_weight(0, wb2)
@@ -216,87 +253,81 @@
     patch_edges(og_t, og_halo)
     part_out[0] = conv_rest(wb2, 1 - f)
     act_pair = send(part_out.at[0], part_in.at[0], pair_s.at[0], pair_r.at[0], to_filter)
-    inp_pair = send(inp_v, pair_inp, field_s.at[1], field_r.at[1], to_filter)
     own_part = conv_rest(wb2, f)
 
-    def send_slices(n, pair, recv):
-        pair.wait_recv()
-        other = recv[...].T
-        if n == 0:
-            other, _ = gelu_pair(other)
-        field_t[n, 1 - f] = other
-        slice_field(n, 1 - f)
-        owned[n, c, 0] = slices[n, c, s]
+    near_edge = lax.broadcasted_iota(jnp.int32, (4, 16, 128), 2) < 64
+
+    def send_edges():
+        above, below = owned[1, 1], owned[1, 0]
+        edge_out[0] = jnp.where(near_edge, pltpu.roll(above[:, 0], 64, 2), above[:, 1])
+        edge_out[1] = jnp.where(near_edge, below[:, 0], pltpu.roll(below[:, 1], 64, 2))
         return [
-            send(
-                slices.at[n, (1 - c) if o else c, (s + k) % 4],
-                owned.at[n, c, (4 - k) % 4],
-                slice_s.at[n, i],
-                slice_r.at[n, i],
-                group_device(k, o),
-            )
-            for i, (k, o) in enumerate(group)
-        ]
-
-    near_edge = lax.broadcasted_iota(jnp.int32, (4, 16, 128), 2) < 64
-
-    def send_edges(n, copies):
-        for copy in copies:
-            copy.wait_recv()
-        above, below = owned[n, 1], owned[n, 0]
-        edge_out[n, 0] = jnp.where(near_edge, pltpu.roll(above[:, 0], 64, 2), above[:, 1])
-        edge_out[n, 1] = jnp.where(near_edge, below[:, 0], pltpu.roll(below[:, 1], 64, 2))
-        return [
-            send(edge_out.at[n, i], edge_in.at[n, i], edge_s.at[n, i], edge_r.at[n, i], device)
+            send(edge_out.at[i], edge_in.at[i], edge_s.at[i], edge_r.at[i], device)
             for i, device in enumerate((to_next_chip, to_last_chip))
         ]
 
-    def make_rhs(n, ref):
-        high, low = parts_of(ref[...].reshape(1024, 128))
-        rhs[n, :, 0:128] = high
-        rhs[n, :, 128:256] = low
-
-    def make_lhs(n, own_planes):
-        near = lanes_of(32) < 64
-
-        def joined(one, two):
-            return pltpu.roll(jnp.where(near, two, one), 64, 1)
-
+    def make_rhs(rhs, value):
+        high, low = parts_of(value)
+        rhs[:, 0:128] = high
+        rhs[:, 128:256] = low
+
+    near = lanes_of(32) < 64
+
+    def joined(one, two):
+        return pltpu.roll(jnp.where(near, two, one), 64, 1)
+
+    def store_shifts(lhs, base, uses):
+        for b in range(3):
+            for e in range(3):
+                value = moved(base, b - 1, e - 1)
+                high = value.astype(BF16).astype(F32)
+                low = value - high
+                for yy in range(4):
+                    rows = slice(yy * 8, yy * 8 + 8)
+                    tile = jnp.concatenate([high[rows], low[rows]], axis=0).astype(BF16)
+                    for a, at in uses:
+                        t = 9 * a + 3 * b + e
+                        lhs[yy, t * 16 : (t + 1) * 16, at] = tile
+
+    def make_act():
         def body(k, carry):
-            first = owned[n, 0, k].reshape(32, 128)
-            last = owned[n, 1, k].reshape(32, 128)
+            at = [pl.ds(pl.multiple_of(k * 384 + n * 128, 128), 128) for n in range(3)]
+            first = owned[0, 0, k].reshape(32, 128)
+            last = owned[0, 1, k].reshape(32, 128)
+            nothing = jnp.zeros((32, 128), F32)
+            store_shifts(lhs_act, joined(nothing, first), ((1, at[0]),))
+            store_shifts(lhs_act, first, ((2, at[0]), (0, at[1])))
+            store_shifts(lhs_act, joined(first, last), ((1, at[1]),))
+            store_shifts(lhs_act, last, ((2, at[1]), (0, at[2])))
+            store_shifts(lhs_act, joined(last, nothing), ((1, at[2]),))
+            return carry
+
+        lax.fori_loop(0, 4, body, 0)
+
+    def make_inp(own_planes):
+        def body(k, carry):
+            at = [pl.ds(pl.multiple_of(n * 512 + k * 128, 128), 128) for n in range(2)]
+            first = owned[1, 0, k].reshape(32, 128)
+            last = owned[1, 1, k].reshape(32, 128)
             if own_planes:
-                bases = [
-                    (first, ((1, 0),)),
-                    (joined(first, last), ((2, 0), (0, 1))),
-                    (last, ((1, 1),)),
-                ]
+                store_shifts(lhs_inp, first, ((1, at[0]),))
+                store_shifts(lhs_inp, joined(first, last), ((2, at[0]), (0, at[1])))
+                store_shifts(lhs_inp, last, ((1, at[1]),))
             else:
-                below, above = edge_in[n, 0, k], edge_in[n, 1, k]
+                below, above = edge_in[0, k], edge_in[1, k]
                 below = jnp.concatenate([pltpu.roll(below, 64, 1), below], axis=0)
                 above = jnp.concatenate([above, pltpu.roll(above, 64, 1)], axis=0)
                 below = jnp.where(chip == 0, 0.0, below)
                 above = jnp.where(chip == 15, 0.0, above)
-                bases = [(joined(below, first), ((0, 0),)), (joined(last, above), ((2, 1),))]
-            for base, uses in bases:
-                for b in range(3):
-                    for e in range(3):
-                        value = moved(base, b - 1, e - 1)
-                        high = value.astype(BF16).astype(F32)
-                        low = value - high
-                        for yy in range(4):
-                            rows = slice(yy * 8, yy * 8 + 8)
-                            tile = jnp.concatenate([high[rows], low[rows]], axis=0).astype(BF16)
-                            for a, core in uses:
-                                t = 9 * a + 3 * b + e
-                                at = pl.ds(pl.multiple_of(core * 512 + k * 128, 128), 128)
-                                lhs[n, yy, t * 16 : (t + 1) * 16, at] = tile
+                store_shifts(lhs_inp, joined(below, first), ((0, at[0]),))
+                store_shifts(lhs_inp, joined(last, above), ((2, at[1]),))
             return carry
 
         lax.fori_loop(0, 4, body, 0)
 
     def raw_chunk(n, k):
-        total = jnp.dot(lhs[n, (y + k) % 4], rhs[n], preferred_element_type=F32)
+        lhs, rhs = (lhs_inp, rhs_pg) if n else (lhs_act, rhs_og)
+        total = jnp.dot(lhs[(y + k) % 4], rhs[...], preferred_element_type=F32)
         total = (total[:, 0:128] + total[:, 128:256]).reshape(TAPS, 16, 128)
         return (total[:, 0:8] + total[:, 8:16]).reshape(ROWS, 128)
 
@@ -310,38 +341,52 @@
         y_sum[n] = raw_chunk(n, 0)
         return copies
 
+    og_all[0, 5 * c] = og_halo[c]
+    rims = [
+        send(og_halo.at[c], og_all.at[(4 - k) % 4, 5 * c], rim_s.at[i], rim_r.at[i], group_device(k, o))
+        for i, (k, o) in enumerate(group)
+    ]
+    pass_slices(1)
+    og_passed = gather_on(og_gather, og_planes, 0)
     loads[4].wait()
     split_weight(1, wb1)
-    og_passed = gather_on(og_gather, og_all, 0)
-    act_slices = send_slices(0, pre_pair, pair_pre)
-    for copy in og_passed:
-        copy.wait_recv()
-    make_rhs(0, og_all)
+    pass_slices(0)
 
     act_pair.wait_recv()
     pg_t = (own_part + part_in[0]) * slope_v[...]
     pgt_v[...] = pg_t
-    pg_v[...] = pg_t.T
-    pg_gather = gather(pg_v, pg_all, 1)
+    pg_v[...] = pg_t.T.reshape(2, 64, 128)
+    pg_gather = gather(pg_v, pg_planes, 1)
     pg_edges = [
-        send(pg_v.at[pl.ds(64, 64)], pg_halo.at[pl.ds(0, 64)], halo_s.at[2], halo_r.at[2], to_next),
-        send(pg_v.at[pl.ds(0, 64)], pg_halo.at[pl.ds(64, 64)], halo_s.at[3], halo_r.at[3], to_last),
+        send(pg_v.at[1], pg_halo.at[0], halo_s.at[2], halo_r.at[2], to_next),
+        send(pg_v.at[0], pg_halo.at[1], halo_s.at[3], halo_r.at[3], to_last),
     ]
     pg_all[c, 0] = pg_v[...]
 
-    act_edges = send_edges(0, act_slices)
-    inp_slices = send_slices(1, inp_pair, pair_inp)
-    make_lhs(0, True)
+    for copy in slice_copies[1]:
+        copy.wait_recv()
+    edges = send_edges()
     patch(pg_t, 1)
     conv_middle(wb1)
-
-    for copy in act_edges:
-        copy.wait_recv()
-    make_lhs(0, False)
+    make_inp(True)
+    for copy in og_passed + rims:
+        copy.wait_recv()
+    planes = lax.broadcasted_iota(jnp.int32, (4, 6, 64, 128), 1)
+    beyond = ((planes == 0) & (chip == 0)) | ((planes == 5) & (chip == 15))
+    make_rhs(rhs_og, jnp.where(beyond, 0.0, og_all[...]).reshape(1536, 128))
+
+    for copy in slice_copies[0]:
+        copy.wait_recv()
+    make_act()
     second_y = raw(0)
-    inp_edges = send_edges(1, inp_slices)
-    make_lhs(1, True)
-    pg_passed = gather_on(pg_gather, pg_all, 1)
+    pg_passed = gather_on(pg_gather, pg_planes, 1)
+    for copy in edges:
+        copy.wait_recv()
+    make_inp(False)
+    for copy in pg_passed:
+        copy.wait_recv()
+    make_rhs(rhs_pg, pg_all[...].reshape(1024, 128))
+    first_y = raw(1)
 
     for copy in pg_edges:
         copy.wait_recv()
@@ -349,14 +394,6 @@
     part_out[1] = conv_rest(wb1, 1 - f)
     in_pair = send(part_out.at[1], part_in.at[1], pair_s.at[1], pair_r.at[1], to_filter)
     own_grad = conv_rest(wb1, f)
-
-    for copy in inp_edges:
-        copy.wait_recv()
-    make_lhs(1, False)
-    for copy in pg_passed:
-        copy.wait_recv()
-    make_rhs(1, pg_all)
-    first_y = raw(1)
 
     def sum_y(n, copies):
         for copy in copies:
@@ -417,7 +454,7 @@
         in_specs=[hbm] * 5,
         out_specs=(vmem, vmem),
         scratch_shapes=[
-            pltpu.VMEM(block, F32),
+            pltpu.VMEM((2, 64, 128), F32),
             pltpu.VMEM(block, F32),
             pltpu.VMEM(block, F32),
             pltpu.VMEM((2, TAPS, 256, 128), F32),
@@ -425,24 +462,25 @@
             pltpu.VMEM((2, 256, K_CONV), BF16),
             pltpu.VMEM((K_CONV, 256), BF16),
             pltpu.VMEM((2, 256, 256), F32),
+            pltpu.VMEM((2, 64, 128), F32),
+            pltpu.VMEM((2, 64, 128), F32),
+            pltpu.VMEM((2, 2, 4, 16, 128), F32),
             pltpu.VMEM(block, F32),
-            pltpu.VMEM(block, F32),
-            pltpu.VMEM(block, F32),
-            pltpu.VMEM(block, F32),
-            pltpu.VMEM(block, F32),
-            pltpu.VMEM((2, 2) + block, F32),
+            pltpu.VMEM((2,) + block, F32),
+            pltpu.VMEM((2, 2, 4, 16, 128), F32),
             pltpu.VMEM((2, 2, 4, 2, 16, 128), F32),
-            pltpu.VMEM((2, 2, 4, 2, 16, 128), F32),
-            pltpu.VMEM((2, 2, 4, 16, 128), F32),
-            pltpu.VMEM((2, 2, 4, 16, 128), F32),
-            pltpu.VMEM((2, 4) + block, F32),
-            pltpu.VMEM((2, 4) + block, F32),
-            pltpu.VMEM((2, 1024, 256), BF16),
-            pltpu.VMEM((2, 4, TAPS * 16, 1024), BF16),
+            pltpu.VMEM((2, 4, 16, 128), F32),
+            pltpu.VMEM((2, 4, 16, 128), F32),
+            pltpu.VMEM((4, 6, 64, 128), F32),
+            pltpu.VMEM((2, 4, 2, 64, 128), F32),
+            pltpu.VMEM((1536, 256), BF16),
+            pltpu.VMEM((1024, 256), BF16),
+            pltpu.VMEM((4, TAPS * 16, 1536), BF16),
+            pltpu.VMEM((4, TAPS * 16, 1024), BF16),
             pltpu.VMEM((2,) + block, F32),
             pltpu.VMEM((2,) + block, F32),
             pltpu.VMEM(block, F32),
-            pltpu.VMEM(block, F32),
+            pltpu.VMEM((2, 64, 128), F32),
             pltpu.VMEM((2, 4, ROWS, 128), F32),
             pltpu.VMEM((2, 4, ROWS, 128), F32),
             pltpu.VMEM((2, ROWS, 128), F32),
@@ -454,8 +492,9 @@
             dma((2,)), dma((2,)),
             dma((2,)), dma((2,)),
             dma((2, 7)), dma((2, 7)),
-            dma((2, 7)), dma((2, 7)),
-            dma((2, 2)), dma((2, 2)),
+            dma((7,)), dma((7,)),
+            dma((2, 2, 7)), dma((2, 2, 7)),
+            dma((2,)), dma((2,)),
             dma((2, 4)), dma((2, 4)),
             dma((2, 4)), dma((2, 4)),
             dma((2, 4)), dma((2, 4)),
@@ -467,7 +506,7 @@
     )(
         inputs.reshape(block),
         pre_gelu.reshape(block),
-        output_grad.reshape(block),
+        output_grad.reshape(2, 64, 128),
         first_weight,
         second_weight,
     )

time: 54.5 us -> 51.7 us (0.949); the launches traced: 53.8 us -> 51.6 us
  Pallas kernels: 53.2 us -> 50.9 us
    pallas_call x1, Pallas kernels: 51.5 us -> 49.2 us  [local(): pl.pallas_call(kernel, out_shape=(jax.ShapeDtypeStruct(block, F32), jax.S...]
where the time goes in v4:
time: 51.7 us; the launch traced here: 51.6 us
  Pallas kernels  50.9 us (98%)
  between operations  0.64 us (1%)
    pallas_call x1, Pallas kernels, local(): pl.pallas_call(kernel, out_shape=(jax.ShapeDtypeStruct(block, F32), jax.S...  49.2 us
    pallas_call x1, Pallas kernels, local(): pl.pallas_call(finish, out_shape=(jax.ShapeDtypeStruct(block, F32), jax.S...  1.71 us

profile of v4, /device:TPU:8, one launch (start us, length us, event | category | flops | bytes accessed | tf_op | source)
XLA Modules:
  0.0 51.6 jit_solution(3643180431931242405)
XLA Ops:
  0.6 49.2 %backward.1 = (f32[128,128]{1,0:T(8,128)}, f32[2,4,56,128]{3,2,1,0:T(8,128)}) custom-call(f32[128,128]{1,0:T(8,128)} %bitcast.6, f32[128,128]{1,0:T(8,128)} %bitcast.7, f32[2,64,128]{2,1,0:T(8,128)} %bitcast.8, f32[27,256,128]{2,1,0:T(8,128)} %w1_hbm.1, f32[27,256,128]{2,1,0:T(8,128)} %w2_hbm.1), custom_call_target="tpu_custom_call" | custom-call | tf_op jit(solution)/shard_map/backward/pallas_call | solution.py:448
  49.9 1.7 %finish.1 = (f32[128,128]{1,0:T(8,128)}, f32[216,128]{1,0:T(8,128)}, f32[216,128]{1,0:T(8,128)}) custom-call(f32[128,128]{1,0:T(8,128)} %get-tuple-element.8.grad_t, f32[2,4,56,128]{3,2,1,0:T(8,128)} %get-tuple-element.9.x_all), custom_call_target="tpu_custom_call" | custom-call | tf_op jit(solution)/shard_map/finish/pallas_call | solution.py:513

commit v5 on v4

--- a/solution.py
+++ b/solution.py
@@ -356,7 +356,10 @@
     pg_t = (own_part + part_in[0]) * slope_v[...]
     pgt_v[...] = pg_t
     pg_v[...] = pg_t.T.reshape(2, 64, 128)
-    pg_gather = gather(pg_v, pg_planes, 1)
+    pg_gather = [
+        send(pg_v, pg_planes((4 - k) % 4), ring_s.at[1, i], ring_r.at[1, i], group_device(k, o))
+        for i, (k, o) in enumerate(group)
+    ]
     pg_edges = [
         send(pg_v.at[1], pg_halo.at[0], halo_s.at[2], halo_r.at[2], to_next),
         send(pg_v.at[0], pg_halo.at[1], halo_s.at[3], halo_r.at[3], to_last),
@@ -379,7 +382,7 @@
         copy.wait_recv()
     make_act()
     second_y = raw(0)
-    pg_passed = gather_on(pg_gather, pg_planes, 1)
+    pg_passed = pg_gather
     for copy in edges:
         copy.wait_recv()
     make_inp(False)
@@ -412,23 +415,33 @@
             copy.wait_recv()
         total = (z_out[n, zl] + z_in[n, 1]) + (z_in[n, 2] + z_in[n, 3])
         x_out[n] = total * (1.0 / 128.0)
-        x_all[n, s] = x_out[n]
+        keep = pltpu.make_async_copy(x_out.at[n], x_all.at[n, s], load_sem.at[n])
+        keep.start()
+        kept.append(keep)
         return [
             send(x_out.at[n], x_all.at[n, s], x_s.at[n, k], x_r.at[n, k], group_device(k, 0))
             for k in (2, 1, 3)
         ]
 
+    kept = []
     second_z = sum_y(0, second_y)
     first_z = sum_y(1, first_y)
     second_x = sum_z(0, second_z)
+    act_pair.wait_send()
     in_pair.wait_recv()
-    grad_out[...] = own_grad + part_in[1]
+    part_out[0] = own_grad + part_in[1]
+    keep = pltpu.make_async_copy(part_out.at[0], grad_out, load_sem.at[2])
+    keep.start()
+    kept.append(keep)
     first_x = sum_z(1, first_z)
     for copy in second_x + first_x:
         copy.wait_recv()
 
     for copy in started:
-        copy.wait_send()
+        if copy is not act_pair:
+            copy.wait_send()
+    for keep in kept:
+        keep.wait()
 
 
 def finish(grad_t, x_all, grad_out, first_out, second_out):
@@ -452,7 +465,7 @@
             jax.ShapeDtypeStruct((2, 4, 56, 128), F32),
         ),
         in_specs=[hbm] * 5,
-        out_specs=(vmem, vmem),
+        out_specs=(hbm, hbm),
         scratch_shapes=[
             pltpu.VMEM((2, 64, 128), F32),
             pltpu.VMEM(block, F32),

time: 51.7 us -> 50.7 us (0.981)
  Pallas kernels: 50.9 us -> 50 us
    pallas_call x1, Pallas kernels: 49.2 us -> 48.3 us  [local(): pl.pallas_call(kernel, out_shape=(jax.ShapeDtypeStruct(block, F32), jax.S...]
where the time goes in v5:
time: 50.7 us; the launch traced here: 50.6 us
  Pallas kernels  50 us (99%)
  between operations  0.64 us (1%)
    pallas_call x1, Pallas kernels, local(): pl.pallas_call(kernel, out_shape=(jax.ShapeDtypeStruct(block, F32), jax.S...  48.3 us
    pallas_call x1, Pallas kernels, local(): pl.pallas_call(finish, out_shape=(jax.ShapeDtypeStruct(block, F32), jax.S...  1.71 us

profile of v5, /device:TPU:8, one launch (start us, length us, event | category | flops | bytes accessed | tf_op | source)
XLA Modules:
  0.0 50.6 jit_solution(9898003893444762300)
XLA Ops:
  0.6 48.3 %backward.1 = (f32[128,128]{1,0:T(8,128)}, f32[2,4,56,128]{3,2,1,0:T(8,128)}) custom-call(f32[128,128]{1,0:T(8,128)} %bitcast.6, f32[128,128]{1,0:T(8,128)} %bitcast.7, f32[2,64,128]{2,1,0:T(8,128)} %bitcast.8, f32[27,256,128]{2,1,0:T(8,128)} %w1_hbm.1, f32[27,256,128]{2,1,0:T(8,128)} %w2_hbm.1), custom_call_target="tpu_custom_call" | custom-call | tf_op jit(solution)/shard_map/backward/pallas_call | solution.py:461
  48.9 1.7 %finish.1 = (f32[128,128]{1,0:T(8,128)}, f32[216,128]{1,0:T(8,128)}, f32[216,128]{1,0:T(8,128)}) custom-call(f32[128,128]{1,0:T(8,128)} %get-tuple-element.8.grad_t, f32[2,4,56,128]{3,2,1,0:T(8,128)} %get-tuple-element.9.x_all), custom_call_target="tpu_custom_call" | custom-call | tf_op jit(solution)/shard_map/finish/pallas_call | solution.py:526

commit v6 on v5

--- a/solution.py
+++ b/solution.py
@@ -429,7 +429,7 @@
     second_x = sum_z(0, second_z)
     act_pair.wait_send()
     in_pair.wait_recv()
-    part_out[0] = own_grad + part_in[1]
+    part_out[0] = (own_grad + part_in[1]).T
     keep = pltpu.make_async_copy(part_out.at[0], grad_out, load_sem.at[2])
     keep.start()
     kept.append(keep)
@@ -445,7 +445,7 @@
 
 
 def finish(grad_t, x_all, grad_out, first_out, second_out):
-    grad_out[...] = grad_t[...].T
+    grad_out[...] = grad_t[...]
     for n, out in ((0, second_out), (1, first_out)):
         for x in range(4):
             for e in range(2):

time: 50.7 us -> 50.7 us (level)
  no operation moved by 1% of the time
where the time goes in v6:
time: 50.7 us; the launch traced here: 50.6 us
  Pallas kernels  50 us (99%)
  between operations  0.64 us (1%)
    pallas_call x1, Pallas kernels, local(): pl.pallas_call(kernel, out_shape=(jax.ShapeDtypeStruct(block, F32), jax.S...  48.3 us
    pallas_call x1, Pallas kernels, local(): pl.pallas_call(finish, out_shape=(jax.ShapeDtypeStruct(block, F32), jax.S...  1.7 us

profile of v6, /device:TPU:8, one launch (start us, length us, event | category | flops | bytes accessed | tf_op | source)
XLA Modules:
  0.0 50.6 jit_solution(12013530389398415089)
XLA Ops:
  0.6 48.3 %backward.1 = (f32[128,128]{1,0:T(8,128)}, f32[2,4,56,128]{3,2,1,0:T(8,128)}) custom-call(f32[128,128]{1,0:T(8,128)} %bitcast.6, f32[128,128]{1,0:T(8,128)} %bitcast.7, f32[2,64,128]{2,1,0:T(8,128)} %bitcast.8, f32[27,256,128]{2,1,0:T(8,128)} %w1_hbm.1, f32[27,256,128]{2,1,0:T(8,128)} %w2_hbm.1), custom_call_target="tpu_custom_call" | custom-call | tf_op jit(solution)/shard_map/backward/pallas_call | solution.py:461
  48.9 1.7 %finish.1 = (f32[128,128]{1,0:T(8,128)}, f32[216,128]{1,0:T(8,128)}, f32[216,128]{1,0:T(8,128)}) custom-call(f32[128,128]{1,0:T(8,128)} %get-tuple-element.8.grad_t, f32[2,4,56,128]{3,2,1,0:T(8,128)} %get-tuple-element.9.x_all), custom_call_target="tpu_custom_call" | custom-call | tf_op jit(solution)/shard_map/finish/pallas_call | solution.py:526
